TPU v7x, 32 devices: a whole 2x2x4 slice. The times are simulated.
32 devices in a mesh: dp: 16 (over z, x, core), tensor: 2 (over y).
Axes of the slice: x: 2, y: 2, z: 4, core: 2. Of those that a mesh axis runs over, the one named last changes fastest.
Arguments:
- tokens: bfloat16 [32768, 768], P('dp'), may hold values from -6 to 6
- lengths: int32 [64], P('dp'), may hold values from 64 to 512, as said below
- w_qkv: bfloat16 [768, 3, 768], P(None, None, 'tensor'), may hold values from -0.21875 to 0.21875
- q_bias: float32 [768], P('tensor'), may hold values from -3 to 3
- v_bias: float32 [768], P('tensor'), may hold values from -3 to 3
- w_out: bfloat16 [768, 768], P('tensor'), may hold values from -0.875 to 0.875
- out_bias: float32 [768], replicated, may hold values from -2 to 2
- gain_one: float32 [768], replicated, may hold values from 0.5 to 1.5
- shift_one: float32 [768], replicated, may hold values from -2 to 2
- w_in: bfloat16 [768, 3072], P(None, 'tensor'), may hold values from -0.21875 to 0.21875
- in_bias: float32 [3072], P('tensor'), may hold values from -3 to 3
- w_down: bfloat16 [3072, 768], P('tensor'), may hold values from -0.15625 to 0.15625
- down_bias: float32 [768], replicated, may hold values from -2 to 2
- gain_two: float32 [768], replicated, may hold values from 0.5 to 1.5
- shift_two: float32 [768], replicated, may hold values from -2 to 2
- cotangent: bfloat16 [32768, 768], P(('dp', 'tensor')), may hold values from -6 to 6
Outputs:
- output: bfloat16 [32768, 768], P(('dp', 'tensor'))
- input_grad: bfloat16 [32768, 768], P(('dp', 'tensor'))
- grad_w_qkv: float32 [768, 3, 768], P(None, None, 'tensor')
- grad_q_bias: float32 [768], P('tensor')
- grad_v_bias: float32 [768], P('tensor')
- grad_w_out: float32 [768, 768], P('tensor')
- grad_out_bias: float32 [768], replicated
- grad_gain_one: float32 [768], replicated
- grad_shift_one: float32 [768], replicated
- grad_w_in: float32 [768, 3072], P(None, 'tensor')
- grad_in_bias: float32 [3072], P('tensor')
- grad_w_down: float32 [3072, 768], P('tensor')
- grad_down_bias: float32 [768], replicated
- grad_gain_two: float32 [768], replicated
- grad_shift_two: float32 [768], replicated
Inputs may be any that keep to these rules, and one draw needn't show every extreme that they name: `lengths`: each sequence's valid tokens are its first ones; at least one sequence has all 512 tokens valid.
All inputs are finite; a program needn't handle non-finite values.
Results may differ from a plain program's by a relative error of at most 0.015.
Values may be sent and summed in bfloat16 or wider, within the bound.
No kernel may reach another device: no remote copies, remote signals or barrier semaphores. Data moves between devices by JAX's collectives and lax.ppermute only.
A program may use at most 192 MiB of HBM per device.

v0:
```python
import jax
import jax.numpy as jnp
from jax import lax
from jax.sharding import PartitionSpec as P

HEAD_DIM = 64


EPSILON = 1e-06
MASKED = -1000000000.0


def layer_norm(values, norm_gain, norm_shift):
    average = jnp.mean(values, axis=-1, keepdims=True)
    centred = values - average
    variance = jnp.mean(centred * centred, axis=-1, keepdims=True)
    return centred * lax.rsqrt(variance + EPSILON) * norm_gain + norm_shift


def exact_gelu(values):
    return jax.nn.gelu(values, approximate=False)


def masked_scores(queries, key_rows, length, score_scale):
    scores = (
        jnp.einsum("qhe,khe->hqk", queries, key_rows, preferred_element_type=jnp.float32)
        * score_scale
    )
    valid = lax.iota(jnp.int32, scores.shape[2]) < length
    return jnp.where(valid[None, None, :], scores, MASKED)


def attend(queries, key_rows, values, length, score_scale):
    scores = masked_scores(queries, key_rows, length, score_scale)
    row_max = jnp.max(scores, axis=-1, keepdims=True)
    exponent = jnp.exp(scores - row_max)
    row_total = jnp.sum(exponent, axis=-1, keepdims=True)
    attn_probs = (exponent / row_total).astype(jnp.bfloat16)
    context = jnp.einsum("hqk,khe->qhe", attn_probs, values, preferred_element_type=jnp.float32)
    return (context, (row_max + jnp.log(row_total))[..., 0])


def attend_back(queries, key_rows, values, length, log_total, grad_context, score_scale):
    scores = masked_scores(queries, key_rows, length, score_scale)
    attn_probs = jnp.exp(scores - log_total[..., None])
    grad_probs = jnp.einsum(
        "qhe,khe->hqk", grad_context, values, preferred_element_type=jnp.float32
    )
    row_inner = jnp.sum(attn_probs * grad_probs, axis=-1, keepdims=True)
    grad_scores = (attn_probs * (grad_probs - row_inner)).astype(jnp.bfloat16)
    grad_queries = (
        jnp.einsum("hqk,khe->qhe", grad_scores, key_rows, preferred_element_type=jnp.float32)
        * score_scale
    )
    grad_keys = (
        jnp.einsum("hqk,qhe->khe", grad_scores, queries, preferred_element_type=jnp.float32)
        * score_scale
    )
    grad_values = jnp.einsum(
        "hqk,qhe->khe",
        attn_probs.astype(jnp.bfloat16),
        grad_context,
        preferred_element_type=jnp.float32,
    )
    return (grad_queries, grad_keys, grad_values)


def body(
    tokens,
    lengths,
    w_qkv,
    q_bias,
    v_bias,
    w_out,
    out_bias,
    gain_one,
    shift_one,
    w_in,
    in_bias,
    w_down,
    down_bias,
    gain_two,
    shift_two,
    cotangent,
):
    seq_count = lengths.shape[0]
    rows_all = tokens.shape[0]
    seq_len = rows_all // seq_count
    local_width = w_qkv.shape[2]
    head_count = local_width // HEAD_DIM
    score_scale = HEAD_DIM ** (-0.5)
    my_rows = cotangent.shape[0]
    offset = lax.axis_index("tensor") * my_rows
    own_inputs = lax.dynamic_slice_in_dim(tokens, offset, my_rows, 0).astype(jnp.float32)

    def split_heads(array):
        return array.reshape(seq_count, seq_len, head_count, HEAD_DIM)

    project = jnp.einsum("td,dcf->tcf", tokens, w_qkv, preferred_element_type=jnp.float32)
    queries = split_heads((project[:, 0] + q_bias).astype(jnp.bfloat16))
    key_rows = split_heads(project[:, 1].astype(jnp.bfloat16))
    values = split_heads((project[:, 2] + v_bias).astype(jnp.bfloat16))

    def forward_one(entries):
        return attend(entries[0], entries[1], entries[2], entries[3], score_scale)

    context, log_total = lax.map(forward_one, (queries, key_rows, values, lengths))
    context = context.reshape(rows_all, local_width).astype(jnp.bfloat16)
    row_block = context
    attended = lax.psum_scatter(
        jnp.dot(row_block, w_out, preferred_element_type=jnp.float32),
        "tensor",
        scatter_dimension=0,
        tiled=True,
    )
    pre_one = attended + out_bias + own_inputs
    hidden_one, norm_one_back = jax.vjp(layer_norm, pre_one, gain_one, shift_one)
    hidden_low = lax.all_gather(hidden_one.astype(jnp.bfloat16), "tensor", axis=0, tiled=True)
    pre_act = jnp.dot(hidden_low, w_in, preferred_element_type=jnp.float32) + in_bias
    activated_full, gelu_back = jax.vjp(exact_gelu, pre_act)
    activated = activated_full.astype(jnp.bfloat16)
    row_block = activated
    branch = lax.psum_scatter(
        jnp.dot(row_block, w_down, preferred_element_type=jnp.float32).astype(jnp.bfloat16),
        "tensor",
        scatter_dimension=0,
        tiled=True,
    ).astype(jnp.float32)
    pre_two = branch + down_bias + hidden_one
    result, norm_two_back = jax.vjp(layer_norm, pre_two, gain_two, shift_two)
    grad_pre_two, grad_gain_two, grad_shift_two = norm_two_back(cotangent.astype(jnp.float32))
    grad_down_bias = jnp.sum(grad_pre_two, axis=0)
    branch_grad = lax.all_gather(grad_pre_two.astype(jnp.bfloat16), "tensor", axis=0, tiled=True)
    grad_w_down = jnp.einsum(
        "tf,td->fd", activated, branch_grad, preferred_element_type=jnp.float32
    )
    grad_act = jnp.einsum("td,fd->tf", branch_grad, w_down, preferred_element_type=jnp.float32)
    grad_pre_act = gelu_back(grad_act)[0].astype(jnp.bfloat16)
    grad_in_bias = jnp.sum(grad_pre_act.astype(jnp.float32), axis=0)
    grad_w_in = jnp.einsum(
        "td,tf->df", hidden_low, grad_pre_act, preferred_element_type=jnp.float32
    )
    row_block = grad_pre_act
    grad_hidden = (
        lax.psum_scatter(
            jnp.einsum("tf,df->td", row_block, w_in, preferred_element_type=jnp.float32),
            "tensor",
            scatter_dimension=0,
            tiled=True,
        )
        + grad_pre_two
    )
    grad_pre_one, grad_gain_one, grad_shift_one = norm_one_back(grad_hidden)
    grad_out_bias = jnp.sum(grad_pre_one, axis=0)
    attended_grad = lax.all_gather(grad_pre_one.astype(jnp.bfloat16), "tensor", axis=0, tiled=True)
    grad_w_out = jnp.einsum("tc,td->cd", context, attended_grad, preferred_element_type=jnp.float32)
    grad_context = jnp.einsum(
        "td,cd->tc", attended_grad, w_out, preferred_element_type=jnp.float32
    ).astype(jnp.bfloat16)

    def backward_one(entries):
        return attend_back(
            entries[0], entries[1], entries[2], entries[3], entries[4], entries[5], score_scale
        )

    grad_queries, grad_keys, grad_values = lax.map(
        backward_one, (queries, key_rows, values, lengths, log_total, split_heads(grad_context))
    )
    grad_queries = grad_queries.reshape(rows_all, local_width).astype(jnp.bfloat16)
    grad_keys = grad_keys.reshape(rows_all, local_width).astype(jnp.bfloat16)
    grad_values = grad_values.reshape(rows_all, local_width).astype(jnp.bfloat16)
    grad_project = jnp.stack([grad_queries, grad_keys, grad_values], axis=1)
    grad_q_bias = jnp.sum(grad_queries.astype(jnp.float32), axis=0)
    grad_v_bias = jnp.sum(grad_values.astype(jnp.float32), axis=0)
    grad_w_qkv = jnp.einsum("td,tcf->dcf", tokens, grad_project, preferred_element_type=jnp.float32)
    row_block = grad_project
    input_grad = (
        lax.psum_scatter(
            jnp.einsum("tcf,dcf->td", row_block, w_qkv, preferred_element_type=jnp.float32).astype(
                jnp.bfloat16
            ),
            "tensor",
            scatter_dimension=0,
            tiled=True,
        ).astype(jnp.float32)
        + grad_pre_one
    )
    row_sums = lax.psum(
        (
            grad_out_bias,
            grad_gain_one,
            grad_shift_one,
            grad_down_bias,
            grad_gain_two,
            grad_shift_two,
        ),
        ("dp", "tensor"),
    )
    summed = lax.psum(
        (grad_w_qkv, grad_q_bias, grad_v_bias, grad_w_out, grad_w_in, grad_in_bias, grad_w_down),
        "dp",
    )
    return (
        result.astype(jnp.bfloat16),
        input_grad.astype(jnp.bfloat16),
        summed[0],
        summed[1],
        summed[2],
        summed[3],
        row_sums[0],
        row_sums[1],
        row_sums[2],
        summed[4],
        summed[5],
        summed[6],
        row_sums[3],
        row_sums[4],
        row_sums[5],
    )


def solution(mesh):
    placed = (
        P("dp", None),
        P("dp"),
        P(None, None, "tensor"),
        P("tensor"),
        P("tensor"),
        P("tensor", None),
        P(),
        P(),
        P(),
        P(None, "tensor"),
        P("tensor"),
        P("tensor", None),
        P(),
        P(),
        P(),
        P(("dp", "tensor"), None),
    )
    return jax.shard_map(
        body,
        mesh=mesh,
        in_specs=placed,
        out_specs=(
            P(("dp", "tensor"), None),
            P(("dp", "tensor"), None),
            P(None, None, "tensor"),
            P("tensor"),
            P("tensor"),
            P("tensor", None),
            P(),
            P(),
            P(),
            P(None, "tensor"),
            P("tensor"),
            P("tensor", None),
            P(),
            P(),
            P(),
        ),
        check_vma=False,
    )
```

profile of v0, /device:TPU:0, one launch (start us, length us, event | category | flops | bytes accessed | tf_op | source)
XLA Modules:
  0.0 992.4 jit_solution(10953542806488711497)
XLA Ops:
  7.2 6.9 fusion.65
  14.2 3.1 fusion.80
  18.6 4.0 copy.49
  22.6 5.2 squeeze.39
  31.6 3.5 copy.50
  35.2 5.2 squeeze.40
  46.9 3.8 convert_element_type.124
  55.0 37.5 %while.26 = (s32[]{:T(128)}, bf16[4,512,6,64]{1,3,2,0:T(8,128)(2,1)}, f32[4,6,512]{2,1,0:T(8,128)}, bf16[4,512,6,64]{1,3,2,0:T(8,128)(2,1)}, s32[4]{0:T(128)S(1)...) while((s32[]{:T(128)}, bf16[4,512,6,64]{1,3,2,0:T(8,128)(2,1)}, ...), condition=%wide.region_3.4_spmd, body=%wide.region_0.3_spmd.sunk | while | flops 421524992 | bytes 20947556 | solution.py:107
  60.9 3.5 fusion.127
  70.2 3.5 fusion.127
  79.6 3.5 fusion.127
  88.9 3.5 fusion.127
  96.8 4.5 fusion.81
  101.4 79.9 %reduce-scatter.5.cloned.1.call-done = f32[1024,768]{1,0:T(8,128)} async-done(((f32[2048,768]{1,0:T(8,128)}), f32[1024,768]{1,0:T(8,128)}) %reduce-scatter.5.cloned.1.call-update) | async-done | bytes 3145744 | tf_op jit(solution)/shard_map/reduce_scatter | solution.py:110
  187.6 45.0 %all-gather.4.cloned.1.call-done = bf16[2048,768]{1,0:T(8,128)(2,1)} async-done(((bf16[1024,768]{1,0:T(8,128)(2,1)}), bf16[2048,768]{1,0:T(8,128)(2,1)}) %all-gather.4.cloned.1.call-update) | async-done | bytes 3145744 | tf_op jit(solution)/shard_map/all_gather | solution.py:118
  232.7 33.9 %multiply_convert_fusion.1 = (bf16[2048,1536]{1,0:T(8,128)(2,1)S(1)}, f32[2048,1536]{1,0:T(8,128)}, f32[2048,1536]{1,0:T(8,128)}) fusion(f32[1536]{0:T(1024)S(1)} %copy-done.36, bf16[2048,768]{1,0:T(8,128)(2,1)} %all-gather.4.cloned.1.call-done, bf16[768,1536]{1,0:T(8,128)(2,1)S(1)} %copy-done), kind=kOutput, calls=%fused_computation.64 | convolution fusion | flops 5039456256 | bytes 36968448 | tf_op jit(solution)/shard_map/dot_general | solution.py:119
  269.2 6.3 convolution_convert_fusion
  275.8 43.2 %reduce-scatter.7.cloned.1.call-done = bf16[1024,768]{1,0:T(8,128)(2,1)} async-done(((bf16[2048,768]{1,0:T(8,128)(2,1)}), bf16[1024,768]{1,0:T(8,128)(2,1)}) %reduce-scatter.7.cloned.1.call-update) | async-done | bytes 1572880 | tf_op jit(solution)/shard_map/reduce_scatter | solution.py:123
  319.1 3.4 fusion.77
  331.9 45.0 %all-gather.6.cloned.1.call-done = bf16[2048,768]{1,0:T(8,128)(2,1)} async-done(((bf16[1024,768]{1,0:T(8,128)(2,1)}), bf16[2048,768]{1,0:T(8,128)(2,1)}) %all-gather.6.cloned.1.call-update) | async-done | bytes 3145744 | tf_op jit(solution)/shard_map/all_gather | solution.py:133
  377.0 16.9 %convert_reduce_fusion = (f32[1536]{0:T(1024)S(1)}, bf16[2048,1536]{1,0:T(8,128)(2,1)S(1)}) fusion(f32[2048,1536]{1,0:T(8,128)} %get-tuple-element.237, bf16[2048,768]{1,0:T(8,128)(2,1)} %all-gather.6.cloned.1.call-done, bf16[1536,768]{1,0:T(8,128)(2,1)} %param.31, f32[2048,1536]{1,0:T(8,128)} %get-tuple-element.251, f32[1536]{0:T(1024)S(1)} %copy-done.36), kind=kOutput, calls=%fused_computation.62 | convolution fusion | flops 4885314048 | bytes 36974592 | tf_op jit(solution)/shard_map/td,fd->tf/dot_general | solution.py:137
  396.6 6.9 fusion.82
  403.6 77.1 %reduce-scatter.9.cloned.1.call-done = f32[1024,768]{1,0:T(8,128)} async-done(((f32[2048,768]{1,0:T(8,128)}), f32[1024,768]{1,0:T(8,128)}) %reduce-scatter.9.cloned.1.call-update) | async-done | bytes 3145744 | tf_op jit(solution)/shard_map/reduce_scatter | solution.py:145
  480.8 4.8 multiply_reduce_fusion.1
  490.7 44.6 %all-gather.8.cloned.1.call-done = bf16[2048,768]{1,0:T(8,128)(2,1)} async-done(((bf16[1024,768]{1,0:T(8,128)(2,1)}), bf16[2048,768]{1,0:T(8,128)(2,1)}) %all-gather.8.cloned.1.call-update) | async-done | bytes 3145744 | tf_op jit(solution)/shard_map/all_gather | solution.py:155
  535.3 4.9 convolution_convert_fusion.1
  542.7 3.8 reshape.193
  553.4 69.1 %while.27 = (s32[]{:T(128)}, bf16[4,512,6,64]{1,3,2,0:T(8,128)(2,1)}, bf16[4,512,6,64]{1,3,2,0:T(8,128)(2,1)}, bf16[4,512,6,64]{1,3,2,0:T(8,128)(2,1)}, bf16[4,5...) while((s32[]{:T(128)}, ...), condition=%wide.region_17.18_spmd, body=%wide.region_15.17_spmd.sunk | while | flops 1030616576 | bytes 83856648 | solution.py:166
  557.6 3.1 multiply_reduce_fusion.6
  574.9 3.1 multiply_reduce_fusion.6
  592.2 3.1 multiply_reduce_fusion.6
  609.4 3.1 multiply_reduce_fusion.6
  622.5 3.8 copy.61
  626.3 3.8 convert_element_type.139
  632.7 3.8 copy.62
  636.4 3.8 convert_element_type.141
  643.0 3.8 copy.63
  646.8 3.8 convert_element_type.143
  653.2 8.9 bitcast_convert_fusion
  662.2 9.8 fusion.85
  671.9 9.7 fusion.84
  685.4 5.8 fusion.68
  691.8 40.9 %all-reduce = (f32[768]{0:T(1024)}, f32[768]{0:T(1024)}, f32[768]{0:T(1024)}, f32[768]{0:T(1024)}, f32[768]{0:T(1024)}, /*index=5*/f32[768]{0:T(1024)}) all-reduce(f32[768]{0:T(1024)S(1)} %get-tuple-element.249, f32[768]{0:T(1024)S(1)} %get-tuple-element.176, ...), channel_id=1, replica_groups=mesh['dp'=16,'tensor'=2] {'dp','tensor'}, use_global_device_ids=true, to_apply=%region_26.27 | all-reduce | flops 4608 | bytes 36864 | tf_op jit(solution)/shard_map/psum | solution.py:188
  735.4 64.2 %all-reduce.1 = (f32[384]{0:T(512)}, f32[384]{0:T(512)}, f32[1536]{0:T(1024)}) all-reduce(f32[384]{0:T(512)S(1)} %reduce_sum.216, f32[384]{0:T(512)S(1)} %reduce_sum.218, f32[1536]{0:T(1024)S(1)} %get-tuple-element.252), channel_id=1, replica_groups=mesh['dp'=16,'tensor'=2] {'dp'}, use_global_device_ids=true, to_apply=%region_21.22 | all-reduce | flops 2304 | bytes 18432 | tf_op jit(solution)/shard_map/psum | solution.py:199
  799.6 4.0 add_convert_fusion.1
  803.6 167.8 %all-reduce.5.cloned.1.call-done = (f32[768,3,384]{0,2,1:T(8,128)}, f32[384,768]{1,0:T(8,128)}, f32[768,1536]{1,0:T(8,128)}, f32[1536,768]{1,0:T(8,128)}) async-done(((f32[768,3,384]{0,2,1:T(8,128)}, f32[384,768]{1,0:T(8,128)}, f32[768,1536]{1,0:T(8,128)}, f32[1536,768]{1,0:T(8,128)}), (f32[768,3,384]{0,2,1:T(8,128)}, f32[384,768]{1,0:T(8,128)}, f32[768,1536]{1,0:T(8,128)}, ...) | async-done | bytes 14155792 | tf_op jit(solution)/shard_map/psum | solution.py:199
  971.4 5.2 copy.68
  977.7 5.5 copy.108
  (230 shorter events, 153.9 us)
Async XLA Ops:
  7.2 225.5 %copy-start = (bf16[768,1536]{1,0:T(8,128)(2,1)S(1)}, bf16[768,1536]{1,0:T(8,128)(2,1)}, u32[]{:S(2)}) copy-start(bf16[768,1536]{1,0:T(8,128)(2,1)} %param.29) | copy-start | bytes 7077892
  7.2 174.1 %reduce-scatter.5.cloned.1.call-start = ((), (), s32[]{:S(2)}) async-start(), calls=%async_computation.4 | async-start | bytes 9437184 | tf_op jit(solution)/shard_map/reduce_scatter | solution.py:110
  22.6 5.2 copy-start.31
  35.2 5.2 copy-start.32
  50.7 4.3 copy-start.37
  92.6 4.3 copy-start.18
  101.4 80.0 %copy-start.28 = (f32[768]{0:T(1024)S(1)}, f32[768]{0:T(1024)}, u32[]{:S(2)}) copy-start(f32[768]{0:T(1024)} %param.26) | copy-start | bytes 9220
  101.4 131.3 %all-gather.4.cloned.1.call-start = ((), (), s32[]{:S(2)}) async-start(), calls=%async_computation.5 | async-start | bytes 4718592 | tf_op jit(solution)/shard_map/all_gather | solution.py:118
  185.8 46.8 %copy-start.36 = (f32[1536]{0:T(1024)S(1)}, f32[1536]{0:T(1024)}, u32[]{:S(2)}) copy-start(f32[1536]{0:T(1024)} %param.30) | copy-start | bytes 18436
  187.6 131.5 %reduce-scatter.7.cloned.1.call-start = ((), (), s32[]{:S(2)}) async-start(), calls=%async_computation.6 | async-start | bytes 4718592 | tf_op jit(solution)/shard_map/reduce_scatter | solution.py:123
  232.7 36.5 %copy-start.35 = (bf16[1536,768]{1,0:T(8,128)(2,1)S(1)}, bf16[1536,768]{1,0:T(8,128)(2,1)}, u32[]{:S(2)}) copy-start(bf16[1536,768]{1,0:T(8,128)(2,1)} %param.31) | copy-start | bytes 7077892
  266.5 2.7 copy-start.39
  275.5 43.5 %copy-start.29 = (f32[768]{0:T(1024)S(1)}, f32[768]{0:T(1024)}, u32[]{:S(2)}) copy-start(f32[768]{0:T(1024)} %param.32) | copy-start | bytes 9220
  275.6 101.4 %all-gather.6.cloned.1.call-start = ((), (), s32[]{:S(2)}) async-start(), calls=%async_computation.7 | async-start | bytes 4718592 | tf_op jit(solution)/shard_map/all_gather | solution.py:133
  323.0 2.6 copy-start.30
  331.9 148.9 %reduce-scatter.9.cloned.1.call-start = ((), (), s32[]{:S(2)}) async-start(), calls=%async_computation.8 | async-start | bytes 9437184 | tf_op jit(solution)/shard_map/reduce_scatter | solution.py:145
  393.9 2.7 copy-start.40
  403.5 82.0 %copy-start.22 = (f32[1024]{0:T(1024)S(1)}, f32[1024]{0:T(1024)}, u32[]{:S(2)}) copy-start(f32[1024]{0:T(1024)} %copy-done.21) | copy-start | bytes 12292
  403.6 131.7 %all-gather.8.cloned.1.call-start = ((), (), s32[]{:S(2)}) async-start(), calls=%async_computation.9 | async-start | bytes 4718592 | tf_op jit(solution)/shard_map/all_gather | solution.py:155
  480.8 4.8 copy-start.2
  488.7 46.6 %copy-start.19 = (bf16[384,768]{1,0:T(8,128)(2,1)S(1)}, bf16[384,768]{1,0:T(8,128)(2,1)}, u32[]{:S(2)}) copy-start(bf16[384,768]{1,0:T(8,128)(2,1)} %param.25) | copy-start | bytes 1769476
  490.2 309.4 %reduce-scatter.11.cloned.1.call-start = ((), (), s32[]{:S(2)}) async-start(), calls=%async_computation.10 | async-start | bytes 4718592 | tf_op jit(solution)/shard_map/reduce_scatter | solution.py:178
  549.4 4.0 copy-start.38
  553.4 4.2 copy-start.7
  560.8 2.2 copy-start.10
  565.2 3.1 copy-start.11
  570.7 4.2 copy-start.7
  578.1 2.2 copy-start.10
  580.3 2.2 copy-start.5
  582.5 3.1 copy-start.11
  588.0 4.2 copy-start.7
  595.3 2.2 copy-start.10
  597.5 2.2 copy-start.5
  599.8 3.1 copy-start.11
  605.2 4.2 copy-start.7
  612.6 2.2 copy-start.10
  617.0 3.1 copy-start.11
  662.1 309.3 %all-reduce.5.cloned.1.call-start = ((), (), s32[]{:S(2)}) async-start(), calls=%async_computation.11 | async-start | bytes 28311552 | tf_op jit(solution)/shard_map/psum | solution.py:199
  662.2 9.8 copy-start.33
  671.9 9.7 copy-start.9
  671.9 9.7 copy-start.34
  681.6 2.5 copy-start.13
  681.6 2.5 copy-start.14
  681.6 2.5 copy-start.15
  681.6 3.7 copy-start.17
  971.4 5.3 copy-start.16
  976.7 6.5 slice-start
  977.7 5.5 slice-start.1
  (18 other events, 24.4 us)
Sparse Core Ops, SparseCore 0:
  101.5 79.7 reduce-scatter.4
  187.7 44.9 all-gather.3
  275.7 43.3 reduce-scatter.6
  332.0 44.9 all-gather.5
  403.7 77.0 reduce-scatter.8
  490.3 44.9 all-gather.7
  662.2 43.8 reduce-scatter.10
  711.9 259.5 all-reduce.4
where the time goes:
time: 998 us; the launch traced here: 992 us
  waiting for transfers between devices  503 us (50%)
  matrix products  189 us (19%)
  local copies, waits for them, and re-layouts  124 us (12%)
  blocking collectives  105 us (11%)
  other arithmetic  55.9 us (6%)
  between operations  14.7 us (1%)
    psum x1, waiting for transfers between devices, body(): lax.psum((grad_w_qkv, grad_q_bias, grad_v_bias, grad_w_out, grad_w_in, gr...  168 us
    reduce_scatter x1, waiting for transfers between devices, body(): lax.psum_scatter(jnp.dot(row_block, w_out, preferred_element_type=jnp.flo...  79.9 us
    reduce_scatter x1, waiting for transfers between devices, body(): lax.psum_scatter(jnp.einsum('tf,df->td', row_block, w_in, preferred_eleme...  77.1 us
    psum x1, blocking collectives, body(): lax.psum((grad_w_qkv, grad_q_bias, grad_v_bias, grad_w_out, grad_w_in, gr...  64.2 us
    all_gather x1, waiting for transfers between devices, body(): lax.all_gather(grad_pre_two.astype(jnp.bfloat16), 'tensor', axis=0, tiled...  45 us
    all_gather x1, waiting for transfers between devices, body(): lax.all_gather(hidden_one.astype(jnp.bfloat16), 'tensor', axis=0, tiled=T...  45 us
    all_gather x1, waiting for transfers between devices, body(): lax.all_gather(grad_pre_one.astype(jnp.bfloat16), 'tensor', axis=0, tiled...  44.6 us
    reduce_scatter x1, waiting for transfers between devices, body(): lax.psum_scatter(jnp.dot(row_block, w_down, preferred_element_type=jnp.fl...  43.2 us
  transfers between devices with their start and end apart: 8, of which 7 were waited for; matrix products, arithmetic and copies ran while one was open for 3% of the time, Pallas kernels for 0%

commit v1 on v0

v1 whole, which is shorter than its diff:
```python
import jax
import jax.numpy as jnp
from jax import lax
from jax.experimental import pallas as pl
from jax.experimental.pallas import tpu as pltpu
from jax.sharding import PartitionSpec as P

HEAD_DIM = 64
EPSILON = 1e-06
MASKED = -1000000000.0
LOW = jnp.bfloat16
WIDE = jnp.float32
RSQRT2 = 0.7071067811865476
RSQRT2PI = 0.3989422804014327


def contract(a, b, dim_a, dim_b):
    return lax.dot_general(
        a, b, (((dim_a,), (dim_b,)), ((), ())), preferred_element_type=WIDE
    )


def halves(d):
    return d & 1, (d >> 1) & 1, (d >> 2) & 1


def swap(array, bit, size):
    return lax.ppermute(array, "dp", [(i, i ^ (1 << bit)) for i in range(size)])


def across(array):
    return lax.ppermute(array, "tensor", [(0, 1), (1, 0)])


def attend_kernel(length_ref, q_ref, k_ref, v_ref, context_ref, probs_ref):
    length = length_ref[pl.program_id(0)]
    rows = q_ref.shape[0]
    lane = lax.broadcasted_iota(jnp.int32, (rows, 128), 1)
    slot = lax.broadcasted_iota(jnp.int32, (rows, 128), 0)
    masked = jnp.where(slot < length, 0.0, MASKED).astype(LOW)
    q, k, v = q_ref[...], k_ref[...], v_ref[...]
    zero, one = jnp.zeros_like(q), jnp.ones_like(q)
    contexts = []
    for head in range(2):
        mine = (lane >= 64) if head else (lane < 64)
        mark = lane == (0 if head else 64)
        k_head = jnp.where(mine, k, jnp.where(mark, masked, zero))
        q_head = jnp.where(mine, q, jnp.where(mark, one, zero))
        scores = contract(k_head, q_head, 1, 1)
        top = jnp.max(scores, axis=0, keepdims=True)
        exponent = jnp.exp(scores - top)
        total = jnp.sum(exponent, axis=0, keepdims=True)
        probs = (exponent * (1.0 / total)).astype(LOW)
        probs_ref[head] = probs
        contexts.append(contract(probs, v, 0, 0))
    context_ref[...] = jnp.where(lane < 64, contexts[0], contexts[1]).astype(LOW)


def attend(lengths, q, k, v):
    rows, width = q.shape
    sequences = lengths.shape[0]
    length, pairs = rows // sequences, width // 128
    block = pl.BlockSpec((length, 128), lambda s, h, *_: (s, h))
    return pl.pallas_call(
        attend_kernel,
        grid_spec=pltpu.PrefetchScalarGridSpec(
            num_scalar_prefetch=1,
            grid=(sequences, pairs),
            in_specs=[block] * 3,
            out_specs=[
                block,
                pl.BlockSpec((2, length, length), lambda s, h, *_: (s * pairs + h, 0, 0)),
            ],
        ),
        out_shape=[
            jax.ShapeDtypeStruct((rows, width), LOW),
            jax.ShapeDtypeStruct((sequences * pairs * 2, length, length), LOW),
        ],
        cost_estimate=pl.CostEstimate(
            flops=11 * 10**9, bytes_accessed=10**7, transcendentals=10**6
        ),
        name="attend",
    )(lengths, q, k, v)


def attend_back_kernel(q_ref, k_ref, v_ref, context_ref, grad_ref, probs_ref, out_ref):
    rows = q_ref.shape[0]
    lane = lax.broadcasted_iota(jnp.int32, (rows, 128), 1)
    q, k, v, grad = q_ref[...], k_ref[...], v_ref[...], grad_ref[...]
    inner = pltpu.roll(grad.astype(WIDE) * context_ref[...].astype(WIDE), 64, 1).astype(LOW)
    zero, minus = jnp.zeros_like(q), -jnp.ones_like(q)
    grad_q = grad_k = grad_v = 0.0
    for head in range(2):
        mine = (lane >= 64) if head else (lane < 64)
        centred = contract(jnp.where(mine, v, minus), jnp.where(mine, grad, inner), 1, 1)
        probs = probs_ref[head]
        grad_scores = (probs.astype(WIDE) * centred).astype(LOW)
        grad_v += contract(probs, jnp.where(mine, grad, zero), 1, 0)
        grad_k += contract(grad_scores, jnp.where(mine, q, zero), 1, 0)
        grad_q += contract(grad_scores, jnp.where(mine, k, zero), 0, 0)
    out_ref[0] = (grad_q * HEAD_DIM**-0.5).astype(LOW)
    out_ref[1] = grad_k.astype(LOW)
    out_ref[2] = grad_v.astype(LOW)


def attend_back(q, k, v, context, grad, probs, sequences):
    rows, width = q.shape
    length, pairs = rows // sequences, width // 128
    block = pl.BlockSpec((length, 128), lambda s, h: (s, h))
    return pl.pallas_call(
        attend_back_kernel,
        grid=(sequences, pairs),
        in_specs=[block] * 5
        + [pl.BlockSpec((2, length, length), lambda s, h: (s * pairs + h, 0, 0))],
        out_specs=pl.BlockSpec((3, length, 128), lambda s, h: (0, s, h)),
        out_shape=jax.ShapeDtypeStruct((3, rows, width), LOW),
        cost_estimate=pl.CostEstimate(
            flops=12 * 10**9, bytes_accessed=10**7, transcendentals=0
        ),
        name="attend_back",
    )(q, k, v, context, grad, probs)


def down_kernel(bits_ref, a_ref, b_ref, *refs):
    out_ref = refs[-1]
    z = bits_ref[2]
    result = contract(a_ref[...], b_ref[...], 0, 0)
    rows = result.shape[0] // 2
    for part in range(2):
        piece = result[part * rows : (part + 1) * rows]
        if len(refs) == 2:
            piece = piece + refs[0][0, part ^ z].astype(WIDE)
        out_ref[0, part ^ z] = piece.astype(LOW)


def down_pieces(bits, send, activated, grad, *received):
    rows, hidden = activated.shape
    width = grad.shape[1]
    block = pl.BlockSpec((1, 2, hidden // 8, width), lambda i, s: (i, 0, 0, 0))
    return pl.pallas_call(
        down_kernel,
        grid_spec=pltpu.PrefetchScalarGridSpec(
            num_scalar_prefetch=1,
            grid=(2,),
            in_specs=[
                pl.BlockSpec((rows, hidden // 4), lambda i, s: (0, (s[0] ^ send) * 2 + (i ^ s[1]))),
                pl.BlockSpec((rows, width), lambda i, s: (0, 0)),
            ]
            + [block] * len(received),
            out_specs=block,
        ),
        out_shape=jax.ShapeDtypeStruct((2, 2, hidden // 8, width), LOW),
        cost_estimate=pl.CostEstimate(flops=3 * 10**9, bytes_accessed=10**6, transcendentals=0),
        name="down_pieces",
    )(bits, activated, grad, *received)


def up_pieces(bits, send, hidden_rows, grad, *received):
    rows, width = hidden_rows.shape
    hidden = grad.shape[1]
    block = pl.BlockSpec((1, 2, width // 2, hidden // 4), lambda i, s: (i, 0, 0, 0))
    return pl.pallas_call(
        down_kernel,
        grid_spec=pltpu.PrefetchScalarGridSpec(
            num_scalar_prefetch=1,
            grid=(2,),
            in_specs=[
                pl.BlockSpec((rows, width), lambda i, s: (0, 0)),
                pl.BlockSpec((rows, hidden // 4), lambda i, s: (0, (s[0] ^ send) * 2 + (i ^ s[1]))),
            ]
            + [block] * len(received),
            out_specs=block,
        ),
        out_shape=jax.ShapeDtypeStruct((2, 2, width // 2, hidden // 4), LOW),
        cost_estimate=pl.CostEstimate(flops=3 * 10**9, bytes_accessed=10**6, transcendentals=0),
        name="up_pieces",
    )(bits, hidden_rows, grad, *received)


def heads_kernel(bits_ref, x_ref, g_ref, context_ref, grad_ref, *refs):
    out_ref = refs[-1]
    mine = bits_ref[1] * 2 + bits_ref[2]

    def put(result):
        rows = result.shape[0] // 4
        for part in range(4):
            piece = result[part * rows : (part + 1) * rows]
            if len(refs) == 2:
                piece = piece + refs[0][part ^ mine, 0].astype(WIDE)
            out_ref[part ^ mine, 0] = piece.astype(LOW)

    @pl.when(pl.program_id(0) < 3)
    def _():
        put(contract(x_ref[...], g_ref[0], 0, 0))

    @pl.when(pl.program_id(0) == 3)
    def _():
        put(contract(context_ref[...], grad_ref[...], 0, 0))


def heads_pieces(bits, send, tokens, grads, context, grad, *received):
    rows, width = tokens.shape
    local = context.shape[1]
    block = pl.BlockSpec((4, 1, width // 8, local), lambda j, s: (0, j, 0, 0))
    return pl.pallas_call(
        heads_kernel,
        grid_spec=pltpu.PrefetchScalarGridSpec(
            num_scalar_prefetch=1,
            grid=(4,),
            in_specs=[
                pl.BlockSpec((rows, width // 2), lambda j, s: (0, s[0] ^ send)),
                pl.BlockSpec((1, rows, local), lambda j, s: (jnp.minimum(j, 2), 0, 0)),
                pl.BlockSpec((rows, local), lambda j, s: (0, 0)),
                pl.BlockSpec((rows, width // 2), lambda j, s: (0, s[0] ^ send)),
            ]
            + [block] * len(received),
            out_specs=block,
        ),
        out_shape=jax.ShapeDtypeStruct((4, 4, width // 8, local), LOW),
        cost_estimate=pl.CostEstimate(flops=3 * 10**9, bytes_accessed=10**6, transcendentals=0),
        name="heads_pieces",
    )(bits, tokens, grads, context, grad, *received)


def add(*arrays):
    total = arrays[0].astype(WIDE)
    for array in arrays[1:]:
        total = total + array.astype(WIDE)
    return total.astype(LOW)


def sum_pieces(own, other, size):
    arrived = across(other)
    here = swap(add(own[1], arrived[1]), 1, size)
    kept = add(own[0], arrived[0], here)
    kept = add(kept[0], swap(kept[1], 2, size))
    for bit in range(3, size.bit_length() - 1):
        kept = add(kept, swap(kept, bit, size))
    pieces = [kept]
    for bit in (2, 1, 0):
        pieces = pieces + [swap(piece, bit, size) for piece in pieces]
    return pieces


def widen_kernel(bits_ref, *refs):
    for index in range(8):

        @pl.when(pl.program_id(0) == index)
        def _():
            refs[-1][...] = refs[index][...].astype(WIDE)


def widen(bits, pieces, shape, block, place):
    def out_place(r, s):
        q = r ^ (s[0] * 4 + s[1] * 2 + s[2])
        return place(q // 4, (q // 2) % 2, q % 2)

    piece = pieces[0].shape
    return pl.pallas_call(
        widen_kernel,
        grid_spec=pltpu.PrefetchScalarGridSpec(
            num_scalar_prefetch=1,
            grid=(8,),
            in_specs=[pl.BlockSpec(piece, lambda r, s: (0,) * len(piece))] * 8,
            out_specs=pl.BlockSpec(block, out_place),
        ),
        out_shape=jax.ShapeDtypeStruct(shape, WIDE),
        name="widen",
    )(bits, *pieces)


def widen_heads_kernel(bits_ref, *refs):
    for index in range(8):

        @pl.when(pl.program_id(0) == index)
        def _():
            refs[-2][...] = refs[index][:3].astype(WIDE)
            refs[-1][...] = refs[index][3].astype(WIDE)


def widen_heads(bits, pieces, width, local):
    def bits_of(r, s):
        q = r ^ (s[0] * 4 + s[1] * 2 + s[2])
        return q // 4, q % 4

    piece = pieces[0].shape
    return pl.pallas_call(
        widen_heads_kernel,
        grid_spec=pltpu.PrefetchScalarGridSpec(
            num_scalar_prefetch=1,
            grid=(8,),
            in_specs=[pl.BlockSpec(piece, lambda r, s: (0,) * len(piece))] * 8,
            out_specs=[
                pl.BlockSpec((3,) + piece[1:], lambda r, s: (0, bits_of(r, s)[0] * 4 + bits_of(r, s)[1], 0)),
                pl.BlockSpec(piece[1:], lambda r, s: (bits_of(r, s)[1], bits_of(r, s)[0])),
            ],
        ),
        out_shape=[
            jax.ShapeDtypeStruct((3, width, local), WIDE),
            jax.ShapeDtypeStruct((local, width), WIDE),
        ],
        name="widen_heads",
    )(bits, *pieces)


def normalize(values):
    average = jnp.mean(values, axis=-1, keepdims=True)
    centred = values - average
    scale = lax.rsqrt(jnp.mean(centred * centred, axis=-1, keepdims=True) + EPSILON)
    return centred * scale, scale


def normalize_back(grad, normed, scale, gain):
    grad_normed = grad * gain
    first = jnp.mean(grad_normed, axis=-1, keepdims=True)
    second = jnp.mean(grad_normed * normed, axis=-1, keepdims=True)
    return scale * (grad_normed - first - normed * second)


def gelu_pair(values):
    below = 0.5 * lax.erfc(-values * RSQRT2)
    density = RSQRT2PI * jnp.exp(-0.5 * values * values)
    return values * below, below + values * density


def fetch(half, axis, core, size):
    extent = half.shape[axis] // 2
    part = lax.dynamic_slice_in_dim(half, core * extent, extent, axis)
    mine = across(part)
    theirs = swap(mine, 0, size)
    return jnp.where(
        core == 0,
        jnp.concatenate([mine, theirs], axis),
        jnp.concatenate([theirs, mine], axis),
    )


def body(
    tokens,
    lengths,
    w_qkv,
    q_bias,
    v_bias,
    w_out,
    out_bias,
    gain_one,
    shift_one,
    w_in,
    in_bias,
    w_down,
    down_bias,
    gain_two,
    shift_two,
    cotangent,
):
    rows, width = cotangent.shape
    seq_len = tokens.shape[0] // lengths.shape[0]
    sequences = rows // seq_len
    local = w_qkv.shape[2]
    hidden = w_in.shape[1]
    size = lax.axis_size("dp")
    pair = lax.axis_index("tensor")
    dp = lax.axis_index("dp")
    core = dp & 1
    bits = jnp.stack(halves(dp)).astype(jnp.int32)

    x = lax.dynamic_slice_in_dim(tokens, pair * rows, rows, 0)
    own_lengths = lax.dynamic_slice_in_dim(lengths, pair * sequences, sequences, 0)

    qkv_own = jnp.transpose(w_qkv, (1, 0, 2))
    qkv_other = fetch(qkv_own, 1, core, size)
    biases = jnp.concatenate([q_bias, v_bias, in_bias])
    biases_other = across(biases)
    out_other = fetch(w_out, 0, core, size)
    in_other = fetch(w_in, 1, core, size)
    down_other = fetch(w_down, 0, core, size)

    def project(weights, biases):
        q = (jnp.dot(x, weights[0], preferred_element_type=WIDE) + biases[:local]).astype(LOW)
        k = jnp.dot(x, weights[1], preferred_element_type=WIDE).astype(LOW)
        v = (jnp.dot(x, weights[2], preferred_element_type=WIDE) + biases[local : 2 * local]).astype(LOW)
        return q * HEAD_DIM**-0.5, k, v

    q_own, k_own, v_own = project(qkv_own, biases)
    context_own, probs_own = attend(own_lengths, q_own, k_own, v_own)
    q_other, k_other, v_other = project(qkv_other, biases_other)
    context_other, probs_other = attend(own_lengths, q_other, k_other, v_other)

    pre_one = (
        jnp.dot(context_own, w_out, preferred_element_type=WIDE)
        + jnp.dot(context_other, out_other, preferred_element_type=WIDE)
        + out_bias
        + x.astype(WIDE)
    )
    normed_one, scale_one = normalize(pre_one)
    hidden_one = normed_one * gain_one + shift_one
    hidden_low = hidden_one.astype(LOW)

    def expand(weights, bias):
        act, slope = gelu_pair(jnp.dot(hidden_low, weights, preferred_element_type=WIDE) + bias)
        return act.astype(LOW), slope.astype(LOW)

    act_own, slope_own = expand(w_in, in_bias)
    act_other, slope_other = expand(in_other, biases_other[2 * local :])
    pre_two = (
        jnp.dot(act_own, w_down, preferred_element_type=WIDE)
        + jnp.dot(act_other, down_other, preferred_element_type=WIDE)
        + down_bias
        + hidden_one
    )
    normed_two, scale_two = normalize(pre_two)
    output = (normed_two * gain_two + shift_two).astype(LOW)

    cot = cotangent.astype(WIDE)
    grad_gain_two = jnp.sum(cot * normed_two, axis=0)
    grad_shift_two = jnp.sum(cot, axis=0)
    grad_pre_two = normalize_back(cot, normed_two, scale_two, gain_two)
    grad_down_bias = jnp.sum(grad_pre_two, axis=0)
    branch_grad = grad_pre_two.astype(LOW)

    def pieces_of(make, other, own):
        sent = swap(make(bits, 1, *other), 0, size)
        other_sum = make(bits, 0, *other, sent)
        sent = swap(make(bits, 1, *own), 0, size)
        own_sum = make(bits, 0, *own, sent)
        return sum_pieces(own_sum, other_sum, size)

    down_grads = pieces_of(down_pieces, (act_other, branch_grad), (act_own, branch_grad))

    def shrink(weights, slope):
        grad_act = contract(branch_grad, weights, 1, 1)
        grad = (grad_act * slope.astype(WIDE)).astype(LOW)
        return grad, jnp.sum(grad.astype(WIDE), axis=0)

    grad_act_other, in_bias_other = shrink(down_other, slope_other)
    grad_act_own, in_bias_own = shrink(w_down, slope_own)
    in_grads = pieces_of(up_pieces, (hidden_low, grad_act_other), (hidden_low, grad_act_own))

    grad_hidden = (
        contract(grad_act_own, w_in, 1, 1) + contract(grad_act_other, in_other, 1, 1) + grad_pre_two
    )
    grad_gain_one = jnp.sum(grad_hidden * normed_one, axis=0)
    grad_shift_one = jnp.sum(grad_hidden, axis=0)
    grad_pre_one = normalize_back(grad_hidden, normed_one, scale_one, gain_one)
    grad_out_bias = jnp.sum(grad_pre_one, axis=0)
    attended_grad = grad_pre_one.astype(LOW)

    def sum_vectors(shared, own, other):
        count = shared.shape[0]
        arrived = across(jnp.concatenate([shared, other]))
        total = jnp.concatenate([shared, own]) + arrived
        for bit in range(size.bit_length() - 1):
            total = total + swap(total, bit, size)
        return total[:count], total[count:]

    shared, grad_in_bias = sum_vectors(
        jnp.concatenate(
            [grad_out_bias, grad_gain_one, grad_shift_one, grad_down_bias, grad_gain_two, grad_shift_two]
        ),
        in_bias_own,
        in_bias_other,
    )
    shared = shared.reshape(6, width)

    context_grad_other = contract(attended_grad, out_other, 1, 1).astype(LOW)
    project_other = attend_back(
        q_other, k_other, v_other, context_other, context_grad_other, probs_other, sequences
    )
    context_grad_own = contract(attended_grad, w_out, 1, 1).astype(LOW)
    project_own = attend_back(q_own, k_own, v_own, context_own, context_grad_own, probs_own, sequences)

    def outer_pieces(bits, send, grads, context, *received):
        pieces = heads_pieces(bits, send, x, grads, context, attended_grad, *received)
        return pieces

    def heads_make(bits, send, grads, context, *received):
        flat = [r.reshape(4, *r.shape[2:]) for r in received]
        out = outer_pieces(bits, send, grads, context, *flat)
        return out.reshape(2, 2, *out.shape[1:])

    heads_grads = pieces_of(
        heads_make, (project_other, context_other), (project_own, context_own)
    )

    def bias_sums(grads):
        return jnp.concatenate(
            [jnp.sum(grads[0].astype(WIDE), axis=0), jnp.sum(grads[2].astype(WIDE), axis=0)]
        )

    _, head_biases = sum_vectors(
        jnp.zeros((0,), WIDE), bias_sums(project_own), bias_sums(project_other)
    )

    input_grad = grad_pre_one
    for grads, weights in ((project_own, qkv_own), (project_other, qkv_other)):
        for index in range(3):
            input_grad = input_grad + contract(grads[index], weights[index], 1, 1)

    grad_w_down = widen(
        bits, down_grads, (hidden, width), down_grads[0].shape, lambda c, i, z: (c * 4 + i * 2 + z, 0)
    )
    grad_w_in = widen(
        bits, in_grads, (width, hidden), in_grads[0].shape, lambda c, i, z: (z, c * 2 + i)
    )
    grad_qkv, grad_w_out = widen_heads(bits, heads_grads, width, local)

    return (
        output,
        input_grad.astype(LOW),
        jnp.transpose(grad_qkv, (1, 0, 2)),
        head_biases[:local],
        head_biases[local:],
        grad_w_out,
        shared[0],
        shared[1],
        shared[2],
        grad_w_in,
        grad_in_bias,
        grad_w_down,
        shared[3],
        shared[4],
        shared[5],
    )


def solution(mesh):
    placed = (
        P("dp", None),
        P("dp"),
        P(None, None, "tensor"),
        P("tensor"),
        P("tensor"),
        P("tensor", None),
        P(),
        P(),
        P(),
        P(None, "tensor"),
        P("tensor"),
        P("tensor", None),
        P(),
        P(),
        P(),
        P(("dp", "tensor"), None),
    )
    return jax.shard_map(
        body,
        mesh=mesh,
        in_specs=placed,
        out_specs=(
            P(("dp", "tensor"), None),
            P(("dp", "tensor"), None),
            P(None, None, "tensor"),
            P("tensor"),
            P("tensor"),
            P("tensor", None),
            P(),
            P(),
            P(),
            P(None, "tensor"),
            P("tensor"),
            P("tensor", None),
            P(),
            P(),
            P(),
        ),
        check_vma=False,
    )
```

time: 998 us -> 476 us (0.48)
  waiting for transfers between devices: 503 us -> 131 us
  Pallas kernels: 0 us -> 130 us
  blocking collectives: 105 us -> 0 us
  local copies, waits for them, and re-layouts: 124 us -> 20.5 us
  matrix products: 189 us -> 119 us
  starting transfers between devices: 1.01 us -> 46.9 us
  other arithmetic: 55.9 us -> 23.1 us
  between operations: 14.7 us -> 1.77 us
    reduce_scatter x4 -> x0, waiting for transfers between devices: 200 us -> none  [the longest x1 79.9 us: body(): lax.psum_scatter(jnp.dot(row_block, w_out, preferred_element_type=jnp.flo...]
    psum x1 -> x0, waiting for transfers between devices: 168 us -> none  [body(): lax.psum((grad_w_qkv, grad_q_bias, grad_v_bias, grad_w_out, grad_w_in, gr...]
    all_gather x3 -> x0, waiting for transfers between devices: 135 us -> none  [the longest x1 45 us: body(): lax.all_gather(grad_pre_two.astype(jnp.bfloat16), 'tensor', axis=0, tiled...]
    ppermute x0 -> x58, waiting for transfers between devices: none -> 131 us  [the longest x10 74.1 us: across(): return lax.ppermute(array, 'tensor', [(0, 1), (1, 0)])]
    pallas_call x0 -> x19, Pallas kernels: none -> 130 us  [the longest x4 25.9 us: heads_pieces(): pl.pallas_call(heads_kernel, grid_spec=pltpu.PrefetchScalarGridSpec(num_s...]
    psum x2 -> x0, blocking collectives: 105 us -> none  [the longest x1 64.2 us: body(): lax.psum((grad_w_qkv, grad_q_bias, grad_v_bias, grad_w_out, grad_w_in, gr...]
    dot_general x40 -> x24, matrix products: 189 us -> 119 us  [the longest x12 48 us: contract(): lax.dot_general(a, b, (((dim_a,), (dim_b,)), ((), ())), preferred_element...]
    ppermute x0 -> x58, starting transfers between devices: none -> 46.9 us  [the longest x48 33.9 us: swap(): return lax.ppermute(array, 'dp', [(i, i ^ 1 << bit) for i in range(size)])]
  transfers between devices with their start and end apart: 8 -> 58, of which waited for: 7 -> 18; matrix products, arithmetic and copies ran while one was open for 3% -> 20% of each run, Pallas kernels for 0% -> 18%
where the time goes in v1:
time: 476 us; the launch traced here: 472 us
  waiting for transfers between devices  131 us (28%)
  Pallas kernels  130 us (27%)
  matrix products  119 us (25%)
  starting transfers between devices  46.9 us (10%)
  other arithmetic  23.1 us (5%)
  local copies, waits for them, and re-layouts  20.5 us (4%)
    ppermute x10, waiting for transfers between devices, across(): return lax.ppermute(array, 'tensor', [(0, 1), (1, 0)])  74.1 us
    ppermute x48, waiting for transfers between devices, swap(): return lax.ppermute(array, 'dp', [(i, i ^ 1 << bit) for i in range(size)])  56.8 us
    dot_general x12, matrix products, contract(): lax.dot_general(a, b, (((dim_a,), (dim_b,)), ((), ())), preferred_element...  48 us
    dot_general x2, matrix products, expand(): jnp.dot(hidden_low, weights, preferred_element_type=WIDE) + bias  38.6 us
    ppermute x48, starting transfers between devices, swap(): return lax.ppermute(array, 'dp', [(i, i ^ 1 << bit) for i in range(size)])  33.9 us
    pallas_call x4, Pallas kernels, heads_pieces(): pl.pallas_call(heads_kernel, grid_spec=pltpu.PrefetchScalarGridSpec(num_s...  25.9 us
    pallas_call x2, Pallas kernels, attend_back(): pl.pallas_call(attend_back_kernel, grid=(sequences, pairs), in_specs=[blo...  22.3 us
    pallas_call x2, Pallas kernels, attend(): pl.pallas_call(attend_kernel, grid_spec=pltpu.PrefetchScalarGridSpec(num_...  21.7 us
  transfers between devices with their start and end apart: 58, of which 18 were waited for; matrix products, arithmetic and copies ran while one was open for 20% of the time, Pallas kernels for 18%

profile of v1, /device:TPU:0, one launch (start us, length us, event | category | flops | bytes accessed | tf_op | source)
XLA Modules:
  0.0 471.6 jit_solution(16001884055777690599)
XLA Ops:
  3.0 3.0 collective-permute-start
  17.9 3.7 convolution_convert_fusion.3.k_ref
  26.8 11.0 %attend.2 = (bf16[1024,384]{1,0:T(8,128)(2,1)}, bf16[12,512,512]{2,1,0:T(8,128)(2,1)}) custom-call(s32[2]{0:T(128)} %dynamic_slice.18.length_ref, bf16[1024,384]{1,0:T(8,128)(2,1)} %fusion.34.q_ref, bf16[1024,384]{1,0:T(8,128)(2,1)} %convolution_convert_fusion.3.k_ref, bf16[1024,384]{1,0:T(8,128)(2,1)} %add_convert_fusion.4.v_ref), custom_call_target="tpu_custom_call" | custom-call | flops 11000000512 | bytes 10000000 | tf_op jit(solution)/shard_map/attend/pallas_call | solution.py:64
  37.8 3.8 fusion.70
  42.8 15.8 %collective-permute-done.5 = bf16[768,768]{1,0:T(8,128)(2,1)} collective-permute-done((bf16[768,768]{1,0:T(8,128)(2,1)}, bf16[768,768]{1,0:T(8,128)(2,1)}, u32[]{:S(2)}, u32[]{:S(2)}) %collective-permute-start.5) | collective-permute-done | bytes 1179680 | tf_op jit(solution)/shard_map/ppermute | solution.py:32
  58.6 24.4 %collective-permute-done.7 = bf16[768,768]{1,0:T(8,128)(2,1)} collective-permute-done((bf16[768,768]{1,0:T(8,128)(2,1)}, bf16[768,768]{1,0:T(8,128)(2,1)}, u32[]{:S(2)}, u32[]{:S(2)}) %collective-permute-start.7) | collective-permute-done | bytes 1179680 | tf_op jit(solution)/shard_map/ppermute | solution.py:32
  85.0 3.9 convolution_convert_fusion.2.k_ref
  92.7 10.7 %attend.3 = (bf16[1024,384]{1,0:T(8,128)(2,1)}, bf16[12,512,512]{2,1,0:T(8,128)(2,1)}) custom-call(s32[2]{0:T(128)} %dynamic_slice.18.length_ref, bf16[1024,384]{1,0:T(8,128)(2,1)} %fusion.40.q_ref, bf16[1024,384]{1,0:T(8,128)(2,1)} %convolution_convert_fusion.2.k_ref, bf16[1024,384]{1,0:T(8,128)(2,1)} %add_convert_fusion.2.v_ref), custom_call_target="tpu_custom_call" | custom-call | flops 11000000512 | bytes 10000000 | tf_op jit(solution)/shard_map/attend/pallas_call | solution.py:64
  104.1 4.0 fusion.68
  110.3 18.5 %multiply_convert_fusion.3 = (bf16[1024,1536]{1,0:T(8,128)(2,1)S(1)}, f32[1024,1536]{1,0:T(8,128)}, f32[1024,1536]{1,0:T(8,128)}) fusion(f32[1536]{0:T(1024)S(1)} %copy-done.49, bf16[1024,768]{1,0:T(8,128)(2,1)S(1)} %fusion.33.a_ref, bf16[768,1536]{1,0:T(8,128)(2,1)S(1)} %copy-done.27), kind=kOutput, calls=%fused_computation.36 | convolution fusion | flops 2519728128 | bytes 19666944 | tf_op jit(solution)/shard_map/dot_general | solution.py:400
  128.8 2.6 fusion.71
  131.5 20.1 %multiply_convert_fusion.2 = (bf16[1024,1536]{1,0:T(8,128)(2,1)S(1)}, f32[1024,1536]{1,0:T(8,128)}, f32[1024,1536]{1,0:T(8,128)}) fusion(f32[1536]{0:T(1024)S(1)} %slice.201, bf16[1024,768]{1,0:T(8,128)(2,1)S(1)} %fusion.33.a_ref, bf16[768,768]{1,0:T(8,128)(2,1)} %collective-permute-done.6, bf16[768,768]{1,0:T(8,128)(2,1)} %collective-permute-done.5, ...), kind=kOutput, calls=%fused_computation.22 | convolution fusion | flops 2530344960 | bytes 19666944 | tf_op jit(solution)/shard_map/dot_general | solution.py:400
  151.6 6.6 %fusion.69 = (f32[1024]{0:T(1024)S(1)}, f32[1024,768]{1,0:T(8,128)S(1)}) fusion(f32[768]{0:T(1024)S(1)} %copy-done.52, f32[768]{0:T(1024)S(1)} %copy-done.48, f32[1024]{0:T(1024)S(1)} %add_rsqrt_fusion.1, f32[1024,768]{1,0:T(8,128)S(1)} %get-tuple-element.71, f32[1024]{0:T(1024)S(1)} %broadcast_multiply_fusion.5, f32[768]{0:T(1024)S(1)} %copy-done.57, ...), kind=kOutput, calls=%fused_computation.188 | convolution fusion | flops 2432826368 | bytes 14963713 | tf_op jit(solution)/shard_map/dot_general | solution.py:407
  166.7 5.0 %down_pieces.6 = bf16[2,2,192,768]{3,2,1,0:T(8,128)(2,1)} custom-call(s32[3]{0:T(128)} %pad_add_fusion.bits_ref, bf16[1024,1536]{1,0:T(8,128)(2,1)} %copy-done.61, bf16[1024,768]{1,0:T(8,128)(2,1)} %convert_element_type.245.b_ref), custom_call_target="tpu_custom_call" | custom-call | flops 3000000000 | bytes 1000000 | tf_op jit(solution)/shard_map/down_pieces/pallas_call | solution.py:140
  171.7 11.9 %convert_reduce_fusion = (f32[1536]{0:T(1024)S(1)}, bf16[1024,1536]{1,0:T(8,128)(2,1)}) fusion(f32[1024,1536]{1,0:T(8,128)} %get-tuple-element.44, f32[1024,1536]{1,0:T(8,128)} %get-tuple-element.73, f32[1536]{0:T(1024)S(1)} %slice.201, bf16[1024,768]{1,0:T(8,128)(2,1)} %convert_element_type.245.b_ref, bf16[768,768]{1,0:T(8,128)(2,1)} %collective-permute-done.8, ...), kind=kOutput, calls=%fused_computation.18 | convolution fusion | flops 2445408768 | bytes 19673088 | tf_op jit(solution)/shard_map/dot_general | solution.py:18
  183.6 5.2 %up_pieces.6 = bf16[2,2,384,384]{3,2,1,0:T(8,128)(2,1)} custom-call(s32[3]{0:T(128)} %pad_add_fusion.bits_ref, bf16[1024,768]{1,0:T(8,128)(2,1)} %copy-done.16, bf16[1024,1536]{1,0:T(8,128)(2,1)} %get-tuple-element.80.b_ref), custom_call_target="tpu_custom_call" | custom-call | flops 3000000000 | bytes 1000000 | tf_op jit(solution)/shard_map/up_pieces/pallas_call | solution.py:162
  188.8 9.4 %convert_reduce_fusion.1 = (f32[1536]{0:T(1024)S(1)}, bf16[1024,1536]{1,0:T(8,128)(2,1)S(1)}) fusion(f32[1024,1536]{1,0:T(8,128)} %get-tuple-element.46, f32[1024,1536]{1,0:T(8,128)} %get-tuple-element.72, f32[1536]{0:T(1024)S(1)} %copy-done.49, bf16[1024,768]{1,0:T(8,128)(2,1)} %convert_element_type.245.b_ref, bf16[1536,768]{1,0:T(8,128)(2,1)} %param.27), kind=kOutput, calls=%fused_computation.19 | convolution fusion | flops 2434791936 | bytes 19673088 | tf_op jit(solution)/shard_map/dot_general | solution.py:18
  199.9 2.6 fusion.72
  202.7 5.8 %multiply_reduce_fusion = (f32[768]{0:T(1024)S(1)}, f32[1024]{0:T(1024)S(1)}, f32[1024]{0:T(1024)S(1)}, f32[768]{0:T(1024)S(1)}, f32[1024,768]{1,0:T(8,128)S(1)}) fusion(f32[1024,768]{1,0:T(8,128)S(1)} %get-tuple-element.71, f32[1024]{0:T(1024)S(1)} %add_rsqrt_fusion.1, f32[1024]{0:T(1024)S(1)} %broadcast_multiply_fusion.5, f32[768]{0:T(1024)S(1)} %copy-done.48, ...), kind=kOutput, calls=%fused_computation.62 | convolution fusion | flops 2435183104 | bytes 18113536 | tf_op jit(solution)/shard_map/dot_general | solution.py:18
  215.4 11.1 %attend_back.3.g_ref = bf16[3,1024,384]{2,1,0:T(8,128)(2,1)} custom-call(bf16[1024,384]{1,0:T(8,128)(2,1)} %fusion.40.q_ref, bf16[1024,384]{1,0:T(8,128)(2,1)} %convolution_convert_fusion.2.k_ref, bf16[1024,384]{1,0:T(8,128)(2,1)} %add_convert_fusion.2.v_ref, bf16[1024,384]{1,0:T(8,128)(2,1)} %get-tuple-element.22.context_ref, ...), custom_call_target="tpu_custom_call" | custom-call | flops 12000000000 | bytes 10000000 | tf_op jit(solution)/shard_map/attend_back/pallas_call | solution.py:110
  228.1 6.4 %heads_pieces.6 = bf16[4,4,96,384]{3,2,1,0:T(8,128)(2,1)} custom-call(s32[3]{0:T(128)} %pad_add_fusion.bits_ref, bf16[1024,768]{1,0:T(8,128)(2,1)} %constant_dynamic-slice_fusion.3.x_ref, bf16[3,1024,384]{2,1,0:T(8,128)(2,1)} %attend_back.3.g_ref, bf16[1024,384]{1,0:T(8,128)(2,1)} %get-tuple-element.22.context_ref, bf16[1024,768]{1,0:T(8,128)(2,1)} %copy-done.17), custom_call_target="tpu_custom_call" | custom-call | flops 3000000000 | bytes 1000000 | tf_op jit(solution)/shard_map/heads_pieces/pallas_call | solution.py:205
  234.5 11.2 %attend_back.2.g_ref = bf16[3,1024,384]{2,1,0:T(8,128)(2,1)} custom-call(bf16[1024,384]{1,0:T(8,128)(2,1)} %fusion.34.q_ref, bf16[1024,384]{1,0:T(8,128)(2,1)} %convolution_convert_fusion.3.k_ref, bf16[1024,384]{1,0:T(8,128)(2,1)} %add_convert_fusion.4.v_ref, bf16[1024,384]{1,0:T(8,128)(2,1)} %get-tuple-element.21.context_ref, ...), custom_call_target="tpu_custom_call" | custom-call | flops 12000000000 | bytes 10000000 | tf_op jit(solution)/shard_map/attend_back/pallas_call | solution.py:110
  247.5 3.8 fusion.42
  254.0 3.8 fusion.43
  258.4 6.4 %heads_pieces.4 = bf16[4,4,96,384]{3,2,1,0:T(8,128)(2,1)} custom-call(s32[3]{0:T(128)} %pad_add_fusion.bits_ref, bf16[1024,768]{1,0:T(8,128)(2,1)} %constant_dynamic-slice_fusion.3.x_ref, bf16[3,1024,384]{2,1,0:T(8,128)(2,1)} %attend_back.2.g_ref, bf16[1024,384]{1,0:T(8,128)(2,1)} %get-tuple-element.21.context_ref, bf16[1024,768]{1,0:T(8,128)(2,1)} %copy-done.17), custom_call_target="tpu_custom_call" | custom-call | flops 3000000000 | bytes 1000000 | tf_op jit(solution)/shard_map/heads_pieces/pallas_call | solution.py:205
  267.0 4.9 %down_pieces.4 = bf16[2,2,192,768]{3,2,1,0:T(8,128)(2,1)} custom-call(s32[3]{0:T(128)} %pad_add_fusion.bits_ref, bf16[1024,1536]{1,0:T(8,128)(2,1)} %copy-done.59, bf16[1024,768]{1,0:T(8,128)(2,1)} %convert_element_type.245.b_ref), custom_call_target="tpu_custom_call" | custom-call | flops 3000000000 | bytes 1000000 | tf_op jit(solution)/shard_map/down_pieces/pallas_call | solution.py:140
  272.4 5.0 %down_pieces.7 = bf16[2,2,192,768]{3,2,1,0:T(8,128)(2,1)} custom-call(s32[3]{0:T(128)} %pad_add_fusion.bits_ref, bf16[1024,1536]{1,0:T(8,128)(2,1)} %copy-done.61, bf16[1024,768]{1,0:T(8,128)(2,1)} %convert_element_type.245.b_ref, bf16[2,2,192,768]{3,2,1,0:T(8,128)(2,1)} %collective-permute-done.46.refs_0_), custom_call_target="tpu_custom_call" | custom-call | flops 3000000000 | bytes 1000000 | tf_op jit(solution)/shard_map/down_pieces/pallas_call | solution.py:140
  279.2 5.3 %up_pieces.4 = bf16[2,2,384,384]{3,2,1,0:T(8,128)(2,1)} custom-call(s32[3]{0:T(128)} %pad_add_fusion.bits_ref, bf16[1024,768]{1,0:T(8,128)(2,1)} %copy-done.16, bf16[1024,1536]{1,0:T(8,128)(2,1)} %copy-done.60), custom_call_target="tpu_custom_call" | custom-call | flops 3000000000 | bytes 1000000 | tf_op jit(solution)/shard_map/up_pieces/pallas_call | solution.py:162
  284.5 5.6 %up_pieces.7 = bf16[2,2,384,384]{3,2,1,0:T(8,128)(2,1)} custom-call(s32[3]{0:T(128)} %pad_add_fusion.bits_ref, bf16[1024,768]{1,0:T(8,128)(2,1)} %copy-done.16, bf16[1024,1536]{1,0:T(8,128)(2,1)} %get-tuple-element.80.b_ref, bf16[2,2,384,384]{3,2,1,0:T(8,128)(2,1)} %collective-permute-done.33.refs_0_), custom_call_target="tpu_custom_call" | custom-call | flops 3000000000 | bytes 1000000 | tf_op jit(solution)/shard_map/up_pieces/pallas_call | solution.py:162
  290.5 6.6 %heads_pieces.7 = bf16[4,4,96,384]{3,2,1,0:T(8,128)(2,1)} custom-call(s32[3]{0:T(128)} %pad_add_fusion.bits_ref, bf16[1024,768]{1,0:T(8,128)(2,1)} %constant_dynamic-slice_fusion.3.x_ref, bf16[3,1024,384]{2,1,0:T(8,128)(2,1)} %attend_back.3.g_ref, bf16[1024,384]{1,0:T(8,128)(2,1)} %get-tuple-element.22.context_ref, bf16[1024,768]{1,0:T(8,128)(2,1)} %copy-done.17, ...), custom_call_target="tpu_custom_call" | custom-call | flops 3000000000 | bytes 1000000 | tf_op jit(solution)/shard_map/heads_pieces/pallas_call | solution.py:205
  298.8 6.6 %heads_pieces.5 = bf16[4,4,96,384]{3,2,1,0:T(8,128)(2,1)} custom-call(s32[3]{0:T(128)} %pad_add_fusion.bits_ref, bf16[1024,768]{1,0:T(8,128)(2,1)} %constant_dynamic-slice_fusion.3.x_ref, bf16[3,1024,384]{2,1,0:T(8,128)(2,1)} %attend_back.2.g_ref, bf16[1024,384]{1,0:T(8,128)(2,1)} %get-tuple-element.21.context_ref, bf16[1024,768]{1,0:T(8,128)(2,1)} %copy-done.17, ...), custom_call_target="tpu_custom_call" | custom-call | flops 3000000000 | bytes 1000000 | tf_op jit(solution)/shard_map/heads_pieces/pallas_call | solution.py:205
  306.9 5.0 %down_pieces.5 = bf16[2,2,192,768]{3,2,1,0:T(8,128)(2,1)} custom-call(s32[3]{0:T(128)} %pad_add_fusion.bits_ref, bf16[1024,1536]{1,0:T(8,128)(2,1)} %copy-done.59, bf16[1024,768]{1,0:T(8,128)(2,1)} %convert_element_type.245.b_ref, bf16[2,2,192,768]{3,2,1,0:T(8,128)(2,1)} %collective-permute-done.45.refs_0_), custom_call_target="tpu_custom_call" | custom-call | flops 3000000000 | bytes 1000000 | tf_op jit(solution)/shard_map/down_pieces/pallas_call | solution.py:140
  315.2 5.4 %up_pieces.5 = bf16[2,2,384,384]{3,2,1,0:T(8,128)(2,1)} custom-call(s32[3]{0:T(128)} %pad_add_fusion.bits_ref, bf16[1024,768]{1,0:T(8,128)(2,1)} %copy-done.16, bf16[1024,1536]{1,0:T(8,128)(2,1)} %copy-done.60, bf16[2,2,384,384]{3,2,1,0:T(8,128)(2,1)} %collective-permute-done.32.refs_0_), custom_call_target="tpu_custom_call" | custom-call | flops 3000000000 | bytes 1000000 | tf_op jit(solution)/shard_map/up_pieces/pallas_call | solution.py:162
  320.6 11.2 %collective-permute-done.34 = bf16[2,2,384,384]{3,2,1,0:T(8,128)(2,1)} collective-permute-done((bf16[2,2,384,384]{3,2,1,0:T(8,128)(2,1)}, bf16[2,2,384,384]{3,2,1,0:T(8,128)(2,1)}, u32[]{:S(2)}, u32[]{:S(2)}) %collective-permute-start.34) | collective-permute-done | bytes 1179680 | tf_op jit(solution)/shard_map/ppermute | solution.py:32
  335.0 21.2 %collective-permute-done.11 = bf16[2,2,4,96,384]{4,3,2,1,0:T(8,128)(2,1)S(1)} collective-permute-done((bf16[2,2,4,96,384]{4,3,2,1,0:T(8,128)(2,1)}, bf16[2,2,4,96,384]{4,3,2,1,0:T(8,128)(2,1)S(1)}, u32[]{:S(2)}, u32[]{:S(2)}) %collective-permute-start.11) | collective-permute-done | bytes 1179680 | tf_op jit(solution)/shard_map/ppermute | solution.py:32
  364.0 8.1 %collective-permute-done.12 = bf16[2,4,96,384]{3,2,1,0:T(8,128)(2,1)S(1)} collective-permute-done((bf16[2,4,96,384]{3,2,1,0:T(8,128)(2,1)S(1)}, bf16[2,4,96,384]{3,2,1,0:T(8,128)(2,1)S(1)}, u32[]{:S(2)}, u32[]{:S(2)}) %collective-permute-start.12) | collective-permute-done | bytes 589856 | tf_op jit(solution)/shard_map/ppermute | solution.py:28
  374.3 2.6 collective-permute-start.50
  376.9 5.4 %collective-permute-done.36 = bf16[384,384]{1,0:T(8,128)(2,1)S(1)} collective-permute-done((bf16[384,384]{1,0:T(8,128)(2,1)S(1)}, bf16[384,384]{1,0:T(8,128)(2,1)S(1)}, u32[]{:S(2)}, u32[]{:S(2)}) %collective-permute-start.36) | collective-permute-done | bytes 294944 | tf_op jit(solution)/shard_map/ppermute | solution.py:28
  383.3 5.2 %collective-permute-done.13 = bf16[4,96,384]{2,1,0:T(8,128)(2,1)S(1)} collective-permute-done((bf16[4,96,384]{2,1,0:T(8,128)(2,1)S(1)}, bf16[4,96,384]{2,1,0:T(8,128)(2,1)S(1)}, u32[]{:S(2)}, u32[]{:S(2)}) %collective-permute-start.13) | collective-permute-done | bytes 294944 | tf_op jit(solution)/shard_map/ppermute | solution.py:28
  389.2 14.9 %collective-permute-done.50 = bf16[192,768]{1,0:T(8,128)(2,1)S(1)} collective-permute-done((bf16[192,768]{1,0:T(8,128)(2,1)S(1)}, bf16[192,768]{1,0:T(8,128)(2,1)S(1)}, u32[]{:S(2)}, u32[]{:S(2)}) %collective-permute-start.50) | collective-permute-done | bytes 294944 | tf_op jit(solution)/shard_map/ppermute | solution.py:28
  406.7 3.1 collective-permute-start.26
  421.5 3.6 collective-permute-done.38.refs_1_
  432.3 5.4 %collective-permute-done.53.refs_3_ = bf16[192,768]{1,0:T(8,128)(2,1)S(1)} collective-permute-done((bf16[192,768]{1,0:T(8,128)(2,1)S(1)}, bf16[192,768]{1,0:T(8,128)(2,1)S(1)}, u32[]{:S(2)}, u32[]{:S(2)}) %collective-permute-start.53) | collective-permute-done | bytes 294944 | tf_op jit(solution)/shard_map/ppermute | solution.py:28
  439.5 2.6 add_convert_fusion
  444.8 5.1 %collective-permute-done.17.refs_3_ = bf16[4,96,384]{2,1,0:T(8,128)(2,1)} collective-permute-done((bf16[4,96,384]{2,1,0:T(8,128)(2,1)}, bf16[4,96,384]{2,1,0:T(8,128)(2,1)}, u32[]{:S(2)}, u32[]{:S(2)}) %collective-permute-start.17) | collective-permute-done | bytes 294944 | tf_op jit(solution)/shard_map/ppermute | solution.py:28
  452.3 6.3 %widen.3 = f32[1536,768]{1,0:T(8,128)} custom-call(s32[3]{0:T(128)} %pad_add_fusion.bits_ref, bf16[192,768]{1,0:T(8,128)(2,1)} %copy-done.20, bf16[192,768]{1,0:T(8,128)(2,1)} %copy-done.29, bf16[192,768]{1,0:T(8,128)(2,1)} %copy-done.30, bf16[192,768]{1,0:T(8,128)(2,1)} %copy-done.35, bf16[192,768]{1,0:T(8,128)(2,1)} %copy-done.32, ...), custom_call_target="tpu_custom_call" | custom-call | tf_op jit(solution)/shard_map/widen/pallas_call | solution.py:259
  458.5 6.1 %widen.2 = f32[768,1536]{1,0:T(8,128)} custom-call(s32[3]{0:T(128)} %pad_add_fusion.bits_ref, bf16[384,384]{1,0:T(8,128)(2,1)} %copy-done.21, bf16[384,384]{1,0:T(8,128)(2,1)} %copy-done.31, bf16[384,384]{1,0:T(8,128)(2,1)} %copy-done.33, bf16[384,384]{1,0:T(8,128)(2,1)} %collective-permute-done.40.refs_3_, bf16[384,384]{1,0:T(8,128)(2,1)} %copy-done.34, ...), custom_call_target="tpu_custom_call" | custom-call | tf_op jit(solution)/shard_map/widen/pallas_call | solution.py:259
  465.4 6.0 %widen_heads.1 = (f32[3,768,384]{2,1,0:T(8,128)}, f32[384,768]{1,0:T(8,128)}) custom-call(s32[3]{0:T(128)} %pad_add_fusion.bits_ref, bf16[4,96,384]{2,1,0:T(8,128)(2,1)} %add_convert_fusion.10.refs_0_, bf16[4,96,384]{2,1,0:T(8,128)(2,1)} %collective-permute-done.15.refs_1_, bf16[4,96,384]{2,1,0:T(8,128)(2,1)} %collective-permute-done.16.refs_2_, ...), custom_call_target="tpu_custom_call" | custom-call | tf_op jit(solution)/shard_map/widen_heads/pallas_call | solution.py:287
  (304 shorter events, 107.9 us)
Async XLA Ops:
  3.0 23.8 %collective-permute-start = (bf16[3,384,384]{2,1,0:T(8,128)(2,1)}, bf16[3,384,384]{2,1,0:T(8,128)(2,1)}, u32[]{:S(2)}, u32[]{:S(2)}) collective-permute-start(bf16[3,384,384]{2,1,0:T(8,128)(2,1)} %dynamic-slice_bitcast_fusion), channel_id=1, source_target_pairs={{0,1},{1,0},{2,3},{3,2},{4,5},{5,4},{6,7},{7,6},{8,9},{9,8},{10,11... | collective-permute-start | bytes 2654216 | tf_op jit(solution)/shard_map/ppermute | solution.py:32
  6.7 35.5 %collective-permute-start.2 = (f32[2304]{0:T(1024)S(1)}, f32[2304]{0:T(1024)S(1)}, u32[]{:S(2)}, u32[]{:S(2)}) collective-permute-start(f32[2304]{0:T(1024)S(1)} %pad_maximum_fusion), channel_id=1, source_target_pairs={{0,1},{1,0},{2,3},{3,2},{4,5},{5,4},{6,7},{7,6},{8,9},{9,8},{10,11... | collective-permute-start | bytes 27656 | tf_op jit(solution)/shard_map/ppermute | solution.py:32
  8.4 33.8 %collective-permute-start.3 = (bf16[192,768]{1,0:T(8,128)(2,1)}, bf16[192,768]{1,0:T(8,128)(2,1)S(1)}, u32[]{:S(2)}, u32[]{:S(2)}) collective-permute-start(bf16[192,768]{1,0:T(8,128)(2,1)} %constant_dynamic-slice_fusion.2), channel_id=1, source_target_pairs={{0,1},{1,0},{2,3},{3,2},{4,5},{5,4},{6,7},{7,6},{8,9},{9,8},{10,11... | collective-permute-start | bytes 884744 | tf_op jit(solution)/shard_map/ppermute | solution.py:32
  12.9 45.7 %collective-permute-start.5 = (bf16[768,768]{1,0:T(8,128)(2,1)}, bf16[768,768]{1,0:T(8,128)(2,1)}, u32[]{:S(2)}, u32[]{:S(2)}) collective-permute-start(bf16[768,768]{1,0:T(8,128)(2,1)} %constant_dynamic-slice_fusion.1), channel_id=1, source_target_pairs={{0,1},{1,0},{2,3},{3,2},{4,5},{5,4},{6,7},{7,6},{8,9},{9,8},{10,11... | collective-permute-start | bytes 3538952 | tf_op jit(solution)/shard_map/ppermute | solution.py:32
  14.0 69.0 %collective-permute-start.7 = (bf16[768,768]{1,0:T(8,128)(2,1)}, bf16[768,768]{1,0:T(8,128)(2,1)}, u32[]{:S(2)}, u32[]{:S(2)}) collective-permute-start(bf16[768,768]{1,0:T(8,128)(2,1)} %constant_dynamic-slice_fusion), channel_id=1, source_target_pairs={{0,1},{1,0},{2,3},{3,2},{4,5},{5,4},{6,7},{7,6},{8,9},{9,8},{10,11... | collective-permute-start | bytes 3538952 | tf_op jit(solution)/shard_map/ppermute | solution.py:32
  26.8 56.3 %collective-permute-start.1 = (bf16[3,384,384]{2,1,0:T(8,128)(2,1)}, bf16[3,384,384]{2,1,0:T(8,128)(2,1)S(1)}, u32[]{:S(2)}, u32[]{:S(2)}) collective-permute-start(bf16[3,384,384]{2,1,0:T(8,128)(2,1)} %collective-permute-done), channel_id=1, source_target_pairs={{0,2},{2,0},{4,6},{6,4},{8,10},{10,8},{12,14},{14,12},{16,18},{18,... | collective-permute-start | bytes 2654216 | tf_op jit(solution)/shard_map/ppermute | solution.py:28
  42.2 61.2 %collective-permute-start.4 = (bf16[192,768]{1,0:T(8,128)(2,1)S(1)}, bf16[192,768]{1,0:T(8,128)(2,1)S(1)}, u32[]{:S(2)}, u32[]{:S(2)}) collective-permute-start(bf16[192,768]{1,0:T(8,128)(2,1)S(1)} %collective-permute-done.3), channel_id=1, source_target_pairs={{0,2},{2,0},{4,6},{6,4},{8,10},{10,8},{12,14},{14,12},{16,18},{18,... | collective-permute-start | bytes 884744 | tf_op jit(solution)/shard_map/ppermute | solution.py:28
  58.6 72.8 %collective-permute-start.6 = (bf16[768,768]{1,0:T(8,128)(2,1)}, bf16[768,768]{1,0:T(8,128)(2,1)}, u32[]{:S(2)}, u32[]{:S(2)}) collective-permute-start(bf16[768,768]{1,0:T(8,128)(2,1)} %collective-permute-done.5), channel_id=1, source_target_pairs={{0,2},{2,0},{4,6},{6,4},{8,10},{10,8},{12,14},{14,12},{16,18},{18,... | collective-permute-start | bytes 3538952 | tf_op jit(solution)/shard_map/ppermute | solution.py:28
  83.1 68.5 %collective-permute-start.8 = (bf16[768,768]{1,0:T(8,128)(2,1)}, bf16[768,768]{1,0:T(8,128)(2,1)}, u32[]{:S(2)}, u32[]{:S(2)}) collective-permute-start(bf16[768,768]{1,0:T(8,128)(2,1)} %collective-permute-done.7), channel_id=1, source_target_pairs={{0,2},{2,0},{4,6},{6,4},{8,10},{10,8},{12,14},{14,12},{16,18},{18,... | collective-permute-start | bytes 3538952 | tf_op jit(solution)/shard_map/ppermute | solution.py:28
  251.3 20.7 %collective-permute-start.46 = (bf16[2,2,192,768]{3,2,1,0:T(8,128)(2,1)}, bf16[2,2,192,768]{3,2,1,0:T(8,128)(2,1)}, u32[]{:S(2)}, u32[]{:S(2)}) collective-permute-start(bf16[2,2,192,768]{3,2,1,0:T(8,128)(2,1)} %down_pieces.6), channel_id=1, source_target_pairs={{0,2},{2,0},{4,6},{6,4},{8,10},{10,8},{12,14},{14,12},{16,18},{18,... | collective-permute-start | bytes 3538952 | tf_op jit(solution)/shard_map/ppermute | solution.py:28
  251.8 32.7 %collective-permute-start.33 = (bf16[2,2,384,384]{3,2,1,0:T(8,128)(2,1)S(1)}, bf16[2,2,384,384]{3,2,1,0:T(8,128)(2,1)}, u32[]{:S(2)}, u32[]{:S(2)}) collective-permute-start(bf16[2,2,384,384]{3,2,1,0:T(8,128)(2,1)S(1)} %copy-done.55), channel_id=1, source_target_pairs={{0,2},{2,0},{4,6},{6,4},{8,10},{10,8},{12,14},{14,12},{16,18},{18,... | collective-permute-start | bytes 3538952 | tf_op jit(solution)/shard_map/ppermute | solution.py:28
  254.0 36.1 %collective-permute-start.10 = (bf16[2,2,4,96,384]{4,3,2,1,0:T(8,128)(2,1)}, bf16[2,2,4,96,384]{4,3,2,1,0:T(8,128)(2,1)}, u32[]{:S(2)}, u32[]{:S(2)}) collective-permute-start(bf16[2,2,4,96,384]{4,3,2,1,0:T(8,128)(2,1)} %bitcast.19), channel_id=1, source_target_pairs={{0,2},{2,0},{4,6},{6,4},{8,10},{10,8},{12,14},{14,12},{16,18},{18,... | collective-permute-start | bytes 3538952 | tf_op jit(solution)/shard_map/ppermute | solution.py:28
  264.8 32.2 %collective-permute-start.9 = (bf16[2,2,4,96,384]{4,3,2,1,0:T(8,128)(2,1)}, bf16[2,2,4,96,384]{4,3,2,1,0:T(8,128)(2,1)}, u32[]{:S(2)}, u32[]{:S(2)}) collective-permute-start(bf16[2,2,4,96,384]{4,3,2,1,0:T(8,128)(2,1)} %bitcast.140), channel_id=1, source_target_pairs={{0,2},{2,0},{4,6},{6,4},{8,10},{10,8},{12,14},{14,12},{16,18},{18,... | collective-permute-start | bytes 3538952 | tf_op jit(solution)/shard_map/ppermute | solution.py:28
  271.9 33.5 %collective-permute-start.45 = (bf16[2,2,192,768]{3,2,1,0:T(8,128)(2,1)}, bf16[2,2,192,768]{3,2,1,0:T(8,128)(2,1)}, u32[]{:S(2)}, u32[]{:S(2)}) collective-permute-start(bf16[2,2,192,768]{3,2,1,0:T(8,128)(2,1)} %down_pieces.4), channel_id=1, source_target_pairs={{0,2},{2,0},{4,6},{6,4},{8,10},{10,8},{12,14},{14,12},{16,18},{18,... | collective-permute-start | bytes 3538952 | tf_op jit(solution)/shard_map/ppermute | solution.py:28
  277.4 34.6 %collective-permute-start.47 = (bf16[2,2,192,768]{3,2,1,0:T(8,128)(2,1)}, bf16[2,2,192,768]{3,2,1,0:T(8,128)(2,1)S(1)}, u32[]{:S(2)}, u32[]{:S(2)}) collective-permute-start(bf16[2,2,192,768]{3,2,1,0:T(8,128)(2,1)} %down_pieces.7), channel_id=1, source_target_pairs={{0,1},{1,0},{2,3},{3,2},{4,5},{5,4},{6,7},{7,6},{8,9},{9,8},{10,11... | collective-permute-start | bytes 3538952 | tf_op jit(solution)/shard_map/ppermute | solution.py:32
  284.4 29.2 %collective-permute-start.32 = (bf16[2,2,384,384]{3,2,1,0:T(8,128)(2,1)}, bf16[2,2,384,384]{3,2,1,0:T(8,128)(2,1)}, u32[]{:S(2)}, u32[]{:S(2)}) collective-permute-start(bf16[2,2,384,384]{3,2,1,0:T(8,128)(2,1)} %up_pieces.4), channel_id=1, source_target_pairs={{0,2},{2,0},{4,6},{6,4},{8,10},{10,8},{12,14},{14,12},{16,18},{18,... | collective-permute-start | bytes 3538952 | tf_op jit(solution)/shard_map/ppermute | solution.py:28
  290.1 41.7 %collective-permute-start.34 = (bf16[2,2,384,384]{3,2,1,0:T(8,128)(2,1)}, bf16[2,2,384,384]{3,2,1,0:T(8,128)(2,1)}, u32[]{:S(2)}, u32[]{:S(2)}) collective-permute-start(bf16[2,2,384,384]{3,2,1,0:T(8,128)(2,1)} %up_pieces.7), channel_id=1, source_target_pairs={{0,1},{1,0},{2,3},{3,2},{4,5},{5,4},{6,7},{7,6},{8,9},{9,8},{10,11... | collective-permute-start | bytes 3538952 | tf_op jit(solution)/shard_map/ppermute | solution.py:32
  297.0 59.2 %collective-permute-start.11 = (bf16[2,2,4,96,384]{4,3,2,1,0:T(8,128)(2,1)}, bf16[2,2,4,96,384]{4,3,2,1,0:T(8,128)(2,1)S(1)}, u32[]{:S(2)}, u32[]{:S(2)}) collective-permute-start(bf16[2,2,4,96,384]{4,3,2,1,0:T(8,128)(2,1)} %bitcast.141), channel_id=1, source_target_pairs={{0,1},{1,0},{2,3},{3,2},{4,5},{5,4},{6,7},{7,6},{8,9},{9,8},{10,11... | collective-permute-start | bytes 3538952 | tf_op jit(solution)/shard_map/ppermute | solution.py:32
  305.4 101.3 %collective-permute-start.25 = (f32[768]{0:T(1024)S(1)}, f32[768]{0:T(1024)S(1)}, u32[]{:S(2)}, u32[]{:S(2)}) collective-permute-start(f32[768]{0:T(1024)S(1)} %add.285), channel_id=1, source_target_pairs={{0,8},{2,10},{4,12},{6,14},{8,0},{10,2},{12,4},{14,6},{16,24},{18,... | collective-permute-start | bytes 9224 | tf_op jit(solution)/shard_map/ppermute | solution.py:28
  312.0 97.7 %collective-permute-start.30 = (f32[6144]{0:T(1024)S(1)}, f32[6144]{0:T(1024)S(1)}, u32[]{:S(2)}, u32[]{:S(2)}) collective-permute-start(f32[6144]{0:T(1024)S(1)} %add.290), channel_id=1, source_target_pairs={{0,8},{2,10},{4,12},{6,14},{8,0},{10,2},{12,4},{14,6},{16,24},{18,... | collective-permute-start | bytes 73736 | tf_op jit(solution)/shard_map/ppermute | solution.py:28
  313.6 45.6 %collective-permute-start.48 = (bf16[2,192,768]{2,1,0:T(8,128)(2,1)S(1)}, bf16[2,192,768]{2,1,0:T(8,128)(2,1)}, u32[]{:S(2)}, u32[]{:S(2)}) collective-permute-start(bf16[2,192,768]{2,1,0:T(8,128)(2,1)S(1)} %fusion.47), channel_id=1, source_target_pairs={{0,4},{2,6},{4,0},{6,2},{8,12},{10,14},{12,8},{14,10},{16,20},{18,... | collective-permute-start | bytes 1769480 | tf_op jit(solution)/shard_map/ppermute | solution.py:28
  333.2 29.0 %collective-permute-start.35 = (bf16[2,384,384]{2,1,0:T(8,128)(2,1)S(1)}, bf16[2,384,384]{2,1,0:T(8,128)(2,1)S(1)}, u32[]{:S(2)}, u32[]{:S(2)}) collective-permute-start(bf16[2,384,384]{2,1,0:T(8,128)(2,1)S(1)} %fusion.46), channel_id=1, source_target_pairs={{0,4},{2,6},{4,0},{6,2},{8,12},{10,14},{12,8},{14,10},{16,20},{18,... | collective-permute-start | bytes 1769480 | tf_op jit(solution)/shard_map/ppermute | solution.py:28
  357.4 14.6 %collective-permute-start.12 = (bf16[2,4,96,384]{3,2,1,0:T(8,128)(2,1)S(1)}, bf16[2,4,96,384]{3,2,1,0:T(8,128)(2,1)S(1)}, u32[]{:S(2)}, u32[]{:S(2)}) collective-permute-start(bf16[2,4,96,384]{3,2,1,0:T(8,128)(2,1)S(1)} %fusion.35), channel_id=1, source_target_pairs={{0,4},{2,6},{4,0},{6,2},{8,12},{10,14},{12,8},{14,10},{16,20},{18,... | collective-permute-start | bytes 1769480 | tf_op jit(solution)/shard_map/ppermute | solution.py:28
  360.5 13.7 %collective-permute-start.49 = (bf16[192,768]{1,0:T(8,128)(2,1)S(1)}, bf16[192,768]{1,0:T(8,128)(2,1)S(1)}, u32[]{:S(2)}, u32[]{:S(2)}) collective-permute-start(bf16[192,768]{1,0:T(8,128)(2,1)S(1)} %slice_bitcast_fusion.36), channel_id=1, source_target_pairs={{0,8},{2,10},{4,12},{6,14},{8,0},{10,2},{12,4},{14,6},{16,24},{18,... | collective-permute-start | bytes 884744 | tf_op jit(solution)/shard_map/ppermute | solution.py:28
  363.5 18.8 %collective-permute-start.36 = (bf16[384,384]{1,0:T(8,128)(2,1)S(1)}, bf16[384,384]{1,0:T(8,128)(2,1)S(1)}, u32[]{:S(2)}, u32[]{:S(2)}) collective-permute-start(bf16[384,384]{1,0:T(8,128)(2,1)S(1)} %slice_bitcast_fusion.38), channel_id=1, source_target_pairs={{0,8},{2,10},{4,12},{6,14},{8,0},{10,2},{12,4},{14,6},{16,24},{18,... | collective-permute-start | bytes 884744 | tf_op jit(solution)/shard_map/ppermute | solution.py:28
  372.3 16.2 %collective-permute-start.13 = (bf16[4,96,384]{2,1,0:T(8,128)(2,1)S(1)}, bf16[4,96,384]{2,1,0:T(8,128)(2,1)S(1)}, u32[]{:S(2)}, u32[]{:S(2)}) collective-permute-start(bf16[4,96,384]{2,1,0:T(8,128)(2,1)S(1)} %slice_bitcast_fusion.40), channel_id=1, source_target_pairs={{0,8},{2,10},{4,12},{6,14},{8,0},{10,2},{12,4},{14,6},{16,24},{18,... | collective-permute-start | bytes 884744 | tf_op jit(solution)/shard_map/ppermute | solution.py:28
  374.3 29.9 %collective-permute-start.50 = (bf16[192,768]{1,0:T(8,128)(2,1)S(1)}, bf16[192,768]{1,0:T(8,128)(2,1)S(1)}, u32[]{:S(2)}, u32[]{:S(2)}) collective-permute-start(bf16[192,768]{1,0:T(8,128)(2,1)S(1)} %fusion.48), channel_id=1, source_target_pairs={{0,16},{2,18},{4,20},{6,22},{8,24},{10,26},{12,28},{14,30},{16,0},... | collective-permute-start | bytes 884744 | tf_op jit(solution)/shard_map/ppermute | solution.py:28
  382.4 28.5 %collective-permute-start.37 = (bf16[384,384]{1,0:T(8,128)(2,1)S(1)}, bf16[384,384]{1,0:T(8,128)(2,1)S(1)}, u32[]{:S(2)}, u32[]{:S(2)}) collective-permute-start(bf16[384,384]{1,0:T(8,128)(2,1)S(1)} %fusion.49), channel_id=1, source_target_pairs={{0,16},{2,18},{4,20},{6,22},{8,24},{10,26},{12,28},{14,30},{16,0},... | collective-permute-start | bytes 884744 | tf_op jit(solution)/shard_map/ppermute | solution.py:28
  388.6 26.6 %collective-permute-start.14 = (bf16[4,96,384]{2,1,0:T(8,128)(2,1)S(1)}, bf16[4,96,384]{2,1,0:T(8,128)(2,1)S(1)}, u32[]{:S(2)}, u32[]{:S(2)}) collective-permute-start(bf16[4,96,384]{2,1,0:T(8,128)(2,1)S(1)} %fusion.50), channel_id=1, source_target_pairs={{0,16},{2,18},{4,20},{6,22},{8,24},{10,26},{12,28},{14,30},{16,0},... | collective-permute-start | bytes 884744 | tf_op jit(solution)/shard_map/ppermute | solution.py:28
  404.2 13.8 %collective-permute-start.51 = (bf16[192,768]{1,0:T(8,128)(2,1)S(1)}, bf16[192,768]{1,0:T(8,128)(2,1)S(1)}, u32[]{:S(2)}, u32[]{:S(2)}) collective-permute-start(bf16[192,768]{1,0:T(8,128)(2,1)S(1)} %add_convert_fusion.8.refs_0_), channel_id=1, source_target_pairs={{0,8},{2,10},{4,12},{6,14},{8,0},{10,2},{12,4},{14,6},{16,24},{18,... | collective-permute-start | bytes 884744 | tf_op jit(solution)/shard_map/ppermute | solution.py:28
  410.9 9.0 %collective-permute-start.52 = (bf16[192,768]{1,0:T(8,128)(2,1)S(1)}, bf16[192,768]{1,0:T(8,128)(2,1)S(1)}, u32[]{:S(2)}, u32[]{:S(2)}) collective-permute-start(bf16[192,768]{1,0:T(8,128)(2,1)S(1)} %add_convert_fusion.8.refs_0_), channel_id=1, source_target_pairs={{0,4},{2,6},{4,0},{6,2},{8,12},{10,14},{12,8},{14,10},{16,20},{18,... | collective-permute-start | bytes 884744 | tf_op jit(solution)/shard_map/ppermute | solution.py:28
  415.2 9.8 %collective-permute-start.38 = (bf16[384,384]{1,0:T(8,128)(2,1)S(1)}, bf16[384,384]{1,0:T(8,128)(2,1)S(1)}, u32[]{:S(2)}, u32[]{:S(2)}) collective-permute-start(bf16[384,384]{1,0:T(8,128)(2,1)S(1)} %add_convert_fusion.9.refs_0_), channel_id=1, source_target_pairs={{0,8},{2,10},{4,12},{6,14},{8,0},{10,2},{12,4},{14,6},{16,24},{18,... | collective-permute-start | bytes 884744 | tf_op jit(solution)/shard_map/ppermute | solution.py:28
  415.2 11.3 %collective-permute-start.39 = (bf16[384,384]{1,0:T(8,128)(2,1)S(1)}, bf16[384,384]{1,0:T(8,128)(2,1)S(1)}, u32[]{:S(2)}, u32[]{:S(2)}) collective-permute-start(bf16[384,384]{1,0:T(8,128)(2,1)S(1)} %add_convert_fusion.9.refs_0_), channel_id=1, source_target_pairs={{0,4},{2,6},{4,0},{6,2},{8,12},{10,14},{12,8},{14,10},{16,20},{18,... | collective-permute-start | bytes 884744 | tf_op jit(solution)/shard_map/ppermute | solution.py:28
  418.0 8.6 %collective-permute-start.41 = (bf16[384,384]{1,0:T(8,128)(2,1)S(1)}, bf16[384,384]{1,0:T(8,128)(2,1)S(1)}, u32[]{:S(2)}, u32[]{:S(2)}) collective-permute-start(bf16[384,384]{1,0:T(8,128)(2,1)S(1)} %add_convert_fusion.9.refs_0_), channel_id=1, source_target_pairs={{0,2},{2,0},{4,6},{6,4},{8,10},{10,8},{12,14},{14,12},{16,18},{18,... | collective-permute-start | bytes 884744 | tf_op jit(solution)/shard_map/ppermute | solution.py:28
  419.9 10.9 %collective-permute-start.15 = (bf16[4,96,384]{2,1,0:T(8,128)(2,1)}, bf16[4,96,384]{2,1,0:T(8,128)(2,1)}, u32[]{:S(2)}, u32[]{:S(2)}) collective-permute-start(bf16[4,96,384]{2,1,0:T(8,128)(2,1)} %add_convert_fusion.10.refs_0_), channel_id=1, source_target_pairs={{0,8},{2,10},{4,12},{6,14},{8,0},{10,2},{12,4},{14,6},{16,24},{18,... | collective-permute-start | bytes 884744 | tf_op jit(solution)/shard_map/ppermute | solution.py:28
  420.7 11.7 %collective-permute-start.16 = (bf16[4,96,384]{2,1,0:T(8,128)(2,1)}, bf16[4,96,384]{2,1,0:T(8,128)(2,1)}, u32[]{:S(2)}, u32[]{:S(2)}) collective-permute-start(bf16[4,96,384]{2,1,0:T(8,128)(2,1)} %add_convert_fusion.10.refs_0_), channel_id=1, source_target_pairs={{0,4},{2,6},{4,0},{6,2},{8,12},{10,14},{12,8},{14,10},{16,20},{18,... | collective-permute-start | bytes 884744 | tf_op jit(solution)/shard_map/ppermute | solution.py:28
  425.1 12.6 %collective-permute-start.53 = (bf16[192,768]{1,0:T(8,128)(2,1)S(1)}, bf16[192,768]{1,0:T(8,128)(2,1)S(1)}, u32[]{:S(2)}, u32[]{:S(2)}) collective-permute-start(bf16[192,768]{1,0:T(8,128)(2,1)S(1)} %collective-permute-done.51.refs_1_), channel_id=1, source_target_pairs={{0,4},{2,6},{4,0},{6,2},{8,12},{10,14},{12,8},{14,10},{16,20},{18,... | collective-permute-start | bytes 884744 | tf_op jit(solution)/shard_map/ppermute | solution.py:28
  426.6 11.1 %collective-permute-start.55 = (bf16[192,768]{1,0:T(8,128)(2,1)S(1)}, bf16[192,768]{1,0:T(8,128)(2,1)S(1)}, u32[]{:S(2)}, u32[]{:S(2)}) collective-permute-start(bf16[192,768]{1,0:T(8,128)(2,1)S(1)} %collective-permute-done.51.refs_1_), channel_id=1, source_target_pairs={{0,2},{2,0},{4,6},{6,4},{8,10},{10,8},{12,14},{14,12},{16,18},{18,... | collective-permute-start | bytes 884744 | tf_op jit(solution)/shard_map/ppermute | solution.py:28
  427.4 11.9 %collective-permute-start.56 = (bf16[192,768]{1,0:T(8,128)(2,1)S(1)}, bf16[192,768]{1,0:T(8,128)(2,1)S(1)}, u32[]{:S(2)}, u32[]{:S(2)}) collective-permute-start(bf16[192,768]{1,0:T(8,128)(2,1)S(1)} %collective-permute-done.52.refs_2_), channel_id=1, source_target_pairs={{0,2},{2,0},{4,6},{6,4},{8,10},{10,8},{12,14},{14,12},{16,18},{18,... | collective-permute-start | bytes 884744 | tf_op jit(solution)/shard_map/ppermute | solution.py:28
  430.8 13.3 %collective-permute-start.40 = (bf16[384,384]{1,0:T(8,128)(2,1)S(1)}, bf16[384,384]{1,0:T(8,128)(2,1)}, u32[]{:S(2)}, u32[]{:S(2)}) collective-permute-start(bf16[384,384]{1,0:T(8,128)(2,1)S(1)} %collective-permute-done.38.refs_1_), channel_id=1, source_target_pairs={{0,4},{2,6},{4,0},{6,2},{8,12},{10,14},{12,8},{14,10},{16,20},{18,... | collective-permute-start | bytes 884744 | tf_op jit(solution)/shard_map/ppermute | solution.py:28
  432.3 11.8 %collective-permute-start.42 = (bf16[384,384]{1,0:T(8,128)(2,1)S(1)}, bf16[384,384]{1,0:T(8,128)(2,1)S(1)}, u32[]{:S(2)}, u32[]{:S(2)}) collective-permute-start(bf16[384,384]{1,0:T(8,128)(2,1)S(1)} %collective-permute-done.38.refs_1_), channel_id=1, source_target_pairs={{0,2},{2,0},{4,6},{6,4},{8,10},{10,8},{12,14},{14,12},{16,18},{18,... | collective-permute-start | bytes 884744 | tf_op jit(solution)/shard_map/ppermute | solution.py:28
  437.7 12.1 %collective-permute-start.17 = (bf16[4,96,384]{2,1,0:T(8,128)(2,1)}, bf16[4,96,384]{2,1,0:T(8,128)(2,1)}, u32[]{:S(2)}, u32[]{:S(2)}) collective-permute-start(bf16[4,96,384]{2,1,0:T(8,128)(2,1)} %collective-permute-done.15.refs_1_), channel_id=1, source_target_pairs={{0,4},{2,6},{4,0},{6,2},{8,12},{10,14},{12,8},{14,10},{16,20},{18,... | collective-permute-start | bytes 884744 | tf_op jit(solution)/shard_map/ppermute | solution.py:28
  439.3 10.6 %collective-permute-start.57 = (bf16[192,768]{1,0:T(8,128)(2,1)S(1)}, bf16[192,768]{1,0:T(8,128)(2,1)S(1)}, u32[]{:S(2)}, u32[]{:S(2)}) collective-permute-start(bf16[192,768]{1,0:T(8,128)(2,1)S(1)} %collective-permute-done.53.refs_3_), channel_id=1, source_target_pairs={{0,2},{2,0},{4,6},{6,4},{8,10},{10,8},{12,14},{14,12},{16,18},{18,... | collective-permute-start | bytes 884744 | tf_op jit(solution)/shard_map/ppermute | solution.py:28
  444.1 20.5 %collective-permute-start.18 = (bf16[4,96,384]{2,1,0:T(8,128)(2,1)}, bf16[4,96,384]{2,1,0:T(8,128)(2,1)}, u32[]{:S(2)}, u32[]{:S(2)}) collective-permute-start(bf16[4,96,384]{2,1,0:T(8,128)(2,1)} %add_convert_fusion.10.refs_0_), channel_id=1, source_target_pairs={{0,2},{2,0},{4,6},{6,4},{8,10},{10,8},{12,14},{14,12},{16,18},{18,... | collective-permute-start | bytes 884744 | tf_op jit(solution)/shard_map/ppermute | solution.py:28
  444.2 20.5 %collective-permute-start.19 = (bf16[4,96,384]{2,1,0:T(8,128)(2,1)}, bf16[4,96,384]{2,1,0:T(8,128)(2,1)}, u32[]{:S(2)}, u32[]{:S(2)}) collective-permute-start(bf16[4,96,384]{2,1,0:T(8,128)(2,1)} %collective-permute-done.15.refs_1_), channel_id=1, source_target_pairs={{0,2},{2,0},{4,6},{6,4},{8,10},{10,8},{12,14},{14,12},{16,18},{18,... | collective-permute-start | bytes 884744 | tf_op jit(solution)/shard_map/ppermute | solution.py:28
  444.7 20.0 %collective-permute-start.20 = (bf16[4,96,384]{2,1,0:T(8,128)(2,1)}, bf16[4,96,384]{2,1,0:T(8,128)(2,1)}, u32[]{:S(2)}, u32[]{:S(2)}) collective-permute-start(bf16[4,96,384]{2,1,0:T(8,128)(2,1)} %collective-permute-done.16.refs_2_), channel_id=1, source_target_pairs={{0,2},{2,0},{4,6},{6,4},{8,10},{10,8},{12,14},{14,12},{16,18},{18,... | collective-permute-start | bytes 884744 | tf_op jit(solution)/shard_map/ppermute | solution.py:28
  449.9 8.7 %collective-permute-start.44 = (bf16[384,384]{1,0:T(8,128)(2,1)}, bf16[384,384]{1,0:T(8,128)(2,1)}, u32[]{:S(2)}, u32[]{:S(2)}) collective-permute-start(bf16[384,384]{1,0:T(8,128)(2,1)} %collective-permute-done.40.refs_3_), channel_id=1, source_target_pairs={{0,2},{2,0},{4,6},{6,4},{8,10},{10,8},{12,14},{14,12},{16,18},{18,... | collective-permute-start | bytes 884744 | tf_op jit(solution)/shard_map/ppermute | solution.py:28
  449.9 14.8 %collective-permute-start.21 = (bf16[4,96,384]{2,1,0:T(8,128)(2,1)}, bf16[4,96,384]{2,1,0:T(8,128)(2,1)S(1)}, u32[]{:S(2)}, u32[]{:S(2)}) collective-permute-start(bf16[4,96,384]{2,1,0:T(8,128)(2,1)} %collective-permute-done.17.refs_3_), channel_id=1, source_target_pairs={{0,2},{2,0},{4,6},{6,4},{8,10},{10,8},{12,14},{14,12},{16,18},{18,... | collective-permute-start | bytes 884744 | tf_op jit(solution)/shard_map/ppermute | solution.py:28
  (73 other events, 750.9 us)

commit v2 on v1

v2 whole, which is shorter than its diff:
```python
import jax
import jax.numpy as jnp
from jax import lax
from jax.experimental import pallas as pl
from jax.experimental.pallas import tpu as pltpu
from jax.sharding import PartitionSpec as P

HEAD_DIM = 64
EPSILON = 1e-06
MASKED = -1000000000.0
LOW = jnp.bfloat16
WIDE = jnp.float32
RSQRT2PI = 0.3989422804014327


def contract(a, b, dim_a, dim_b):
    return lax.dot_general(
        a, b, (((dim_a,), (dim_b,)), ((), ())), preferred_element_type=WIDE
    )


def halves(d):
    return d & 1, (d >> 1) & 1, (d >> 2) & 1


def swap(array, bit, size):
    return lax.ppermute(array, "dp", [(i, i ^ (1 << bit)) for i in range(size)])


def across(array):
    return lax.ppermute(array, "tensor", [(0, 1), (1, 0)])


def attend_kernel(length_ref, q_ref, k_ref, v_ref, context_ref, probs_ref):
    length = length_ref[pl.program_id(0)]
    rows = q_ref.shape[0]
    lane = lax.broadcasted_iota(jnp.int32, (rows, 128), 1)
    slot = lax.broadcasted_iota(jnp.int32, (rows, 128), 0)
    masked = jnp.where(slot < length, 0.0, MASKED).astype(LOW)
    q, k, v = q_ref[...], k_ref[...], v_ref[...]
    zero, one = jnp.zeros_like(q), jnp.ones_like(q)
    contexts = []
    for head in range(2):
        mine = (lane >= 64) if head else (lane < 64)
        mark = lane == (0 if head else 64)
        k_head = jnp.where(mine, k, jnp.where(mark, masked, zero))
        q_head = jnp.where(mine, q, jnp.where(mark, one, zero))
        scores = contract(k_head, q_head, 1, 1)
        top = jnp.max(scores, axis=0, keepdims=True)
        exponent = jnp.exp(scores - top)
        total = jnp.sum(exponent, axis=0, keepdims=True)
        probs = (exponent * (1.0 / total)).astype(LOW)
        probs_ref[head] = probs
        contexts.append(contract(probs, v, 0, 0))
    context_ref[...] = jnp.where(lane < 64, contexts[0], contexts[1]).astype(LOW)


def attend(lengths, q, k, v):
    rows, width = q.shape
    sequences = lengths.shape[0]
    length, pairs = rows // sequences, width // 128
    block = pl.BlockSpec((length, 128), lambda s, h, *_: (s, h))
    return pl.pallas_call(
        attend_kernel,
        grid_spec=pltpu.PrefetchScalarGridSpec(
            num_scalar_prefetch=1,
            grid=(sequences, pairs),
            in_specs=[block] * 3,
            out_specs=[
                block,
                pl.BlockSpec((2, length, length), lambda s, h, *_: (s * pairs + h, 0, 0)),
            ],
        ),
        out_shape=[
            jax.ShapeDtypeStruct((rows, width), LOW),
            jax.ShapeDtypeStruct((sequences * pairs * 2, length, length), LOW),
        ],
        cost_estimate=small_cost(),
        name="attend",
    )(lengths, q, k, v)


def attend_back_kernel(q_ref, k_ref, v_ref, context_ref, grad_ref, probs_ref, out_ref):
    rows = q_ref.shape[0]
    lane = lax.broadcasted_iota(jnp.int32, (rows, 128), 1)
    q, k, v, grad = q_ref[...], k_ref[...], v_ref[...], grad_ref[...]
    inner = pltpu.roll(grad.astype(WIDE) * context_ref[...].astype(WIDE), 64, 1).astype(LOW)
    zero, minus = jnp.zeros_like(q), -jnp.ones_like(q)
    grad_q = grad_k = grad_v = 0.0
    for head in range(2):
        mine = (lane >= 64) if head else (lane < 64)
        centred = contract(jnp.where(mine, v, minus), jnp.where(mine, grad, inner), 1, 1)
        probs = probs_ref[head]
        grad_scores = (probs.astype(WIDE) * centred).astype(LOW)
        grad_v += contract(probs, jnp.where(mine, grad, zero), 1, 0)
        grad_k += contract(grad_scores, jnp.where(mine, q, zero), 1, 0)
        grad_q += contract(grad_scores, jnp.where(mine, k, zero), 0, 0)
    out_ref[0] = (grad_q * HEAD_DIM**-0.5).astype(LOW)
    out_ref[1] = grad_k.astype(LOW)
    out_ref[2] = grad_v.astype(LOW)


def attend_back(q, k, v, context, grad, probs, sequences):
    rows, width = q.shape
    length, pairs = rows // sequences, width // 128
    block = pl.BlockSpec((length, 128), lambda s, h: (s, h))
    return pl.pallas_call(
        attend_back_kernel,
        grid=(sequences, pairs),
        in_specs=[block] * 5
        + [pl.BlockSpec((2, length, length), lambda s, h: (s * pairs + h, 0, 0))],
        out_specs=pl.BlockSpec((3, length, 128), lambda s, h: (0, s, h)),
        out_shape=jax.ShapeDtypeStruct((3, rows, width), LOW),
        cost_estimate=small_cost(),
        name="attend_back",
    )(q, k, v, context, grad, probs)


def fetch(piece, size):
    here = across(piece)
    pieces = [here, swap(here, 2, size), swap(here, 1, size)]
    pieces.append(swap(pieces[1], 1, size))
    return pieces + [swap(part, 0, size) for part in pieces]


def rank_of(bits_ref):
    return bits_ref[0] * 4 + bits_ref[1] * 2 + bits_ref[2]


class Loads:
    def __init__(self, semaphores):
        self.semaphores, self.count, self.groups = semaphores, 0, []

    def group(self, pairs):
        copies = []
        for source, target in pairs:
            copies.append(pltpu.make_async_copy(source, target, self.semaphores.at[self.count]))
            self.count += 1
        self.groups.append(copies)
        return len(self.groups) - 1

    def start(self):
        @pl.when(pl.program_id(0) == 0)
        def _():
            for copies in self.groups:
                for copy in copies:
                    copy.start()

    def wait(self, group):
        @pl.when(pl.program_id(0) == 0)
        def _():
            for copy in self.groups[group]:
                copy.wait()


def tall(ref, start, extent):
    return ref.at[pl.ds(pl.multiple_of(start, 16), extent)]


def qkv_parts(parts, target, rank):
    extent = target.shape[1] // 8
    return [
        (part.at[:3], target.at[:, pl.ds(pl.multiple_of((r ^ rank) * extent, 16), extent)])
        for r, part in enumerate(parts)
    ]


def out_parts(parts, target, rank):
    extent, width = target.shape[0] // 8, target.shape[1] // 2
    return [
        (
            part.at[3, pl.ds(side * extent, extent)],
            target.at[pl.ds(pl.multiple_of((r ^ rank) * extent, 16), extent), pl.ds(side * width, width)],
        )
        for r, part in enumerate(parts)
        for side in range(2)
    ]


def in_parts(parts, target, rank):
    extent, width = target.shape[0] // 8, target.shape[1] // 2
    return [
        (
            part.at[pl.ds(side * extent, extent)],
            target.at[pl.ds(pl.multiple_of((r ^ rank) * extent, 16), extent), pl.ds(side * width, width)],
        )
        for r, part in enumerate(parts)
        for side in range(2)
    ]


def down_parts(parts, target, rank):
    extent = target.shape[0] // 8
    return [
        (part.at[pl.ds(extent, extent)], target.at[pl.ds(pl.multiple_of((r ^ rank) * extent, 16), extent)])
        for r, part in enumerate(parts)
    ]


ANYWHERE = pl.BlockSpec(memory_space=pl.ANY)


def small_cost(flops=10**6):
    return pl.CostEstimate(flops=flops, bytes_accessed=10**5, transcendentals=0)


def project_kernel(bits_ref, x_ref, q_bias_ref, v_bias_ref, *refs):
    parts, (q_ref, k_ref, v_ref, weights, semaphores) = refs[:-5], refs[-5:]
    loads = Loads(semaphores)
    if len(parts) == 1:
        ready = loads.group([(parts[0], weights)])
    else:
        ready = loads.group(qkv_parts(parts, weights, rank_of(bits_ref)))
    loads.start()
    loads.wait(ready)
    x = x_ref[...]
    queries = (contract(x, weights[0], 1, 0) + q_bias_ref[...]).astype(LOW)
    q_ref[...] = queries * HEAD_DIM**-0.5
    k_ref[...] = contract(x, weights[1], 1, 0).astype(LOW)
    v_ref[...] = (contract(x, weights[2], 1, 0) + v_bias_ref[...]).astype(LOW)


def project(bits, tokens, row_start, rows, local, biases, parts):
    width = tokens.shape[1]
    tile = 256
    return pl.pallas_call(
        project_kernel,
        grid_spec=pltpu.PrefetchScalarGridSpec(
            num_scalar_prefetch=1,
            grid=(rows // tile,),
            in_specs=[
                pl.BlockSpec((tile, width), lambda i, s: (i, 0)),
                pl.BlockSpec((1, local), lambda i, s: (0, 0)),
                pl.BlockSpec((1, local), lambda i, s: (0, 1)),
            ]
            + [ANYWHERE] * len(parts),
            out_specs=[pl.BlockSpec((tile, local), lambda i, s: (i, 0))] * 3,
            scratch_shapes=[pltpu.VMEM((3, width, local), LOW), pltpu.SemaphoreType.DMA((8,))],
        ),
        out_shape=[jax.ShapeDtypeStruct((rows, local), LOW)] * 3,
        cost_estimate=small_cost(),
        name="project",
    )(bits, tokens, biases, biases, *parts)


def project_back_kernel(bits_ref, own_ref, other_ref, grad_ref, weights_ref, *refs):
    parts, (out_ref, own_weights, other_weights, semaphores) = refs[:-4], refs[-4:]
    loads = Loads(semaphores)
    own_ready = loads.group([(weights_ref, own_weights)])
    other_ready = loads.group(qkv_parts(parts, other_weights, rank_of(bits_ref)))
    loads.start()
    loads.wait(own_ready)
    total = grad_ref[...].astype(WIDE)
    for index in range(3):
        total += contract(own_ref[index], own_weights[index], 1, 1)
    loads.wait(other_ready)
    for index in range(3):
        total += contract(other_ref[index], other_weights[index], 1, 1)
    out_ref[...] = total.astype(LOW)


def project_back(bits, own, other, grad, weights, parts):
    rows, width = grad.shape
    local = own.shape[2]
    tile = 256
    block = pl.BlockSpec((3, tile, local), lambda i, s: (0, i, 0))
    row_block = pl.BlockSpec((tile, width), lambda i, s: (i, 0))
    return pl.pallas_call(
        project_back_kernel,
        grid_spec=pltpu.PrefetchScalarGridSpec(
            num_scalar_prefetch=1,
            grid=(rows // tile,),
            in_specs=[block, block, row_block] + [ANYWHERE] * (1 + len(parts)),
            out_specs=row_block,
            scratch_shapes=[pltpu.VMEM((3, width, local), LOW)] * 2 + [pltpu.SemaphoreType.DMA((9,))],
        ),
        out_shape=jax.ShapeDtypeStruct((rows, width), LOW),
        cost_estimate=small_cost(),
        name="project_back",
    )(bits, own, other, grad, weights, *parts)


def normalize(values):
    average = jnp.mean(values, axis=-1, keepdims=True)
    centred = values - average
    scale = lax.rsqrt(jnp.mean(centred * centred, axis=-1, keepdims=True) + EPSILON)
    return centred * scale, scale


def normalize_back(grad, normed, scale, gain):
    grad_normed = grad * gain
    first = jnp.mean(grad_normed, axis=-1, keepdims=True)
    second = jnp.mean(grad_normed * normed, axis=-1, keepdims=True)
    return scale * (grad_normed - first - normed * second)


TAIL = (
    0.0356748104095459,
    -0.15720322728157043,
    0.20635373890399933,
    -0.053683843463659286,
    0.12856172025203705,
    0.09991346299648285,
    0.12075395882129669,
    0.11962930113077164,
)


def gelu_pair(values):
    t = 1.0 / (1.0 + 0.3 * jnp.abs(values))
    bell = jnp.exp(-0.5 * (values * values))
    series = TAIL[0]
    for coefficient in TAIL[1:]:
        series = series * t + coefficient
    tail = bell * (t * series)
    below = jnp.where(values < 0.0, tail, 1.0 - tail)
    return values * below, below + RSQRT2PI * (values * bell)


def first_kernel(
    bits_ref,
    own_context_ref,
    other_context_ref,
    x_ref,
    out_bias_ref,
    gain_ref,
    shift_ref,
    down_bias_ref,
    in_bias_ref,
    w_out_ref,
    w_in_ref,
    w_down_ref,
    *refs,
):
    parts = refs[:8]
    hidden_ref, normed_ref, scale_ref, base_ref, act_ref, slope_ref = refs[8:14]
    own_out, other_out, w_in, w_down, semaphores = refs[14:]
    loads = Loads(semaphores)
    out_ready = loads.group([(w_out_ref, own_out)] + out_parts(parts, other_out, rank_of(bits_ref)))
    in_ready = loads.group([(w_in_ref, w_in)])
    down_ready = loads.group([(w_down_ref, w_down)])
    loads.start()
    loads.wait(out_ready)
    pre_one = contract(own_context_ref[...], own_out[...], 1, 0)
    pre_one += contract(other_context_ref[...], other_out[...], 1, 0)
    pre_one += out_bias_ref[...] + x_ref[...].astype(WIDE)
    normed, scale = normalize(pre_one)
    hidden = normed * gain_ref[...] + shift_ref[...]
    hidden_low = hidden.astype(LOW)
    hidden_ref[...] = hidden_low
    normed_ref[...] = normed.astype(LOW)
    scale_ref[...] = scale
    loads.wait(in_ready)
    act, slope = gelu_pair(contract(hidden_low, w_in[...], 1, 0) + in_bias_ref[...])
    act = act.astype(LOW)
    act_ref[...] = act
    slope_ref[...] = slope.astype(LOW)
    loads.wait(down_ready)
    base_ref[...] = hidden + down_bias_ref[...] + contract(act, w_down[...], 1, 0)


def first_half(bits, own_context, other_context, x, vectors, in_bias, w_out, w_in, w_down, parts):
    rows, width = x.shape
    local, hidden = own_context.shape[1], w_in.shape[1]
    tile = 256

    def row_block(columns):
        return pl.BlockSpec((tile, columns), lambda i, s: (i, 0))

    def whole(columns):
        return pl.BlockSpec((1, columns), lambda i, s: (0, 0))

    return pl.pallas_call(
        first_kernel,
        grid_spec=pltpu.PrefetchScalarGridSpec(
            num_scalar_prefetch=1,
            grid=(rows // tile,),
            in_specs=[row_block(local), row_block(local), row_block(width)]
            + [whole(width)] * 4
            + [whole(hidden)]
            + [ANYWHERE] * (3 + len(parts)),
            out_specs=[
                row_block(width),
                row_block(width),
                row_block(1),
                row_block(width),
                row_block(hidden),
                row_block(hidden),
            ],
            scratch_shapes=[
                pltpu.VMEM((local, width), LOW),
                pltpu.VMEM((local, width), LOW),
                pltpu.VMEM((width, hidden), LOW),
                pltpu.VMEM((hidden, width), LOW),
                pltpu.SemaphoreType.DMA((19,)),
            ],
        ),
        out_shape=[
            jax.ShapeDtypeStruct((rows, width), LOW),
            jax.ShapeDtypeStruct((rows, width), LOW),
            jax.ShapeDtypeStruct((rows, 1), WIDE),
            jax.ShapeDtypeStruct((rows, width), WIDE),
            jax.ShapeDtypeStruct((rows, hidden), LOW),
            jax.ShapeDtypeStruct((rows, hidden), LOW),
        ],
        cost_estimate=small_cost(),
        name="first_half",
    )(bits, own_context, other_context, x, *vectors, in_bias, w_out, w_in, w_down, *parts)


def second_kernel(
    bits_ref,
    hidden_ref,
    base_ref,
    cot_ref,
    slope_ref,
    normed_ref,
    scale_ref,
    gain_one_ref,
    gain_two_ref,
    shift_two_ref,
    in_bias_ref,
    w_out_ref,
    w_in_ref,
    w_down_ref,
    *refs,
):
    out_pieces, pieces = refs[:8], refs[8:16]
    output_ref, branch_ref, act_ref, own_grad_ref, other_grad_ref, attended_ref = refs[16:22]
    own_context_ref, other_context_ref, sums_ref, bias_sums_ref = refs[22:26]
    own_out, other_out, own_in, other_in, own_down, other_down, semaphores = refs[26:]
    rank = rank_of(bits_ref)
    loads = Loads(semaphores)
    other_in_ready = loads.group(in_parts(pieces, other_in, rank))
    other_down_ready = loads.group(down_parts(pieces, other_down, rank))
    own_down_ready = loads.group([(w_down_ref, own_down)])
    own_in_ready = loads.group([(w_in_ref, own_in)])
    out_ready = loads.group([(w_out_ref, own_out)] + out_parts(out_pieces, other_out, rank))
    loads.start()

    @pl.when(pl.program_id(0) == 0)
    def _():
        sums_ref[...] = jnp.zeros_like(sums_ref)
        bias_sums_ref[...] = jnp.zeros_like(bias_sums_ref)

    def count(ref, row, values):
        ref[row : row + 1] += jnp.sum(values, axis=0, keepdims=True)

    loads.wait(other_in_ready)
    act, slope = gelu_pair(contract(hidden_ref[...], other_in[...], 1, 0) + in_bias_ref[...])
    act = act.astype(LOW)
    act_ref[...] = act
    loads.wait(other_down_ready)
    pre_two = base_ref[...] + contract(act, other_down[...], 1, 0)
    normed, scale = normalize(pre_two)
    output_ref[...] = (normed * gain_two_ref[...] + shift_two_ref[...]).astype(LOW)
    cot = cot_ref[...].astype(WIDE)
    grad_pre_two = normalize_back(cot, normed, scale, gain_two_ref[...])
    count(sums_ref, 4, cot * normed)
    count(sums_ref, 5, cot)
    count(sums_ref, 3, grad_pre_two)
    branch_grad = grad_pre_two.astype(LOW)
    branch_ref[...] = branch_grad
    grad = contract(branch_grad, other_down[...], 1, 1) * slope
    count(bias_sums_ref, 1, grad)
    grad = grad.astype(LOW)
    other_grad_ref[...] = grad
    grad_hidden = grad_pre_two + contract(grad, other_in[...], 1, 1)
    loads.wait(own_down_ready)
    grad = contract(branch_grad, own_down[...], 1, 1) * slope_ref[...].astype(WIDE)
    count(bias_sums_ref, 0, grad)
    grad = grad.astype(LOW)
    own_grad_ref[...] = grad
    loads.wait(own_in_ready)
    grad_hidden += contract(grad, own_in[...], 1, 1)
    normed = normed_ref[...].astype(WIDE)
    grad_pre_one = normalize_back(grad_hidden, normed, scale_ref[...], gain_one_ref[...])
    count(sums_ref, 1, grad_hidden * normed)
    count(sums_ref, 2, grad_hidden)
    count(sums_ref, 0, grad_pre_one)
    attended = grad_pre_one.astype(LOW)
    attended_ref[...] = attended
    loads.wait(out_ready)
    own_context_ref[...] = contract(attended, own_out[...], 1, 1).astype(LOW)
    other_context_ref[...] = contract(attended, other_out[...], 1, 1).astype(LOW)


def second_half(bits, hidden_low, base, cot, slope, normed, scale, vectors, in_bias, w_out, w_in, w_down, out_pieces, pieces):
    rows, width = hidden_low.shape
    local, hidden = w_out.shape[0], w_in.shape[1]
    tile = 256

    def row_block(columns):
        return pl.BlockSpec((tile, columns), lambda i, s: (i, 0))

    def whole(columns, count=1):
        return pl.BlockSpec((count, columns), lambda i, s: (0, 0))

    def low(columns):
        return jax.ShapeDtypeStruct((rows, columns), LOW)

    return pl.pallas_call(
        second_kernel,
        grid_spec=pltpu.PrefetchScalarGridSpec(
            num_scalar_prefetch=1,
            grid=(rows // tile,),
            in_specs=[
                row_block(width),
                row_block(width),
                row_block(width),
                row_block(hidden),
                row_block(width),
                row_block(1),
            ]
            + [whole(width)] * 3
            + [whole(hidden)]
            + [ANYWHERE] * 19,
            out_specs=[
                row_block(width),
                row_block(width),
                row_block(hidden),
                row_block(hidden),
                row_block(hidden),
                row_block(width),
                row_block(local),
                row_block(local),
                whole(width, 8),
                whole(hidden, 8),
            ],
            scratch_shapes=[
                pltpu.VMEM((local, width), LOW),
                pltpu.VMEM((local, width), LOW),
                pltpu.VMEM((width, hidden), LOW),
                pltpu.VMEM((width, hidden), LOW),
                pltpu.VMEM((hidden, width), LOW),
                pltpu.VMEM((hidden, width), LOW),
                pltpu.SemaphoreType.DMA((43,)),
            ],
        ),
        out_shape=[
            low(width),
            low(width),
            low(hidden),
            low(hidden),
            low(hidden),
            low(width),
            low(local),
            low(local),
            jax.ShapeDtypeStruct((8, width), WIDE),
            jax.ShapeDtypeStruct((8, hidden), WIDE),
        ],
        cost_estimate=small_cost(),
        name="second_half",
    )(bits, hidden_low, base, cot, slope, normed, scale, *vectors, in_bias, w_out, w_in, w_down, *out_pieces, *pieces)


def down_kernel(bits_ref, act_ref, grad_ref, sent_ref, kept_ref):
    z = bits_ref[2]
    result = contract(act_ref[...], grad_ref[...], 0, 0)
    rows = result.shape[0] // 2

    def put(out_ref):
        for part in range(2):
            out_ref[0, part ^ z] = result[part * rows : (part + 1) * rows].astype(LOW)

    @pl.when(pl.program_id(0) < 2)
    def _():
        put(sent_ref)

    @pl.when(pl.program_id(0) >= 2)
    def _():
        put(kept_ref)


def down_pieces(bits, activated, grad):
    rows, hidden = activated.shape
    width = grad.shape[1]
    piece = (1, 2, hidden // 8, width)
    return pl.pallas_call(
        down_kernel,
        grid_spec=pltpu.PrefetchScalarGridSpec(
            num_scalar_prefetch=1,
            grid=(4,),
            in_specs=[
                pl.BlockSpec(
                    (rows, hidden // 4), lambda i, s: (0, (s[0] ^ (1 - i // 2)) * 2 + ((i % 2) ^ s[1]))
                ),
                pl.BlockSpec((rows, width), lambda i, s: (0, 0)),
            ],
            out_specs=[
                pl.BlockSpec(piece, lambda i, s: (jnp.minimum(i, 1), 0, 0, 0)),
                pl.BlockSpec(piece, lambda i, s: (jnp.maximum(i - 2, 0), 0, 0, 0)),
            ],
        ),
        out_shape=[jax.ShapeDtypeStruct((2,) + piece[1:], LOW)] * 2,
        cost_estimate=small_cost(),
        name="down_pieces",
    )(bits, activated, grad)


def in_kernel(bits_ref, hidden_ref, grad_ref, sent_ref, kept_ref):
    x, z = bits_ref[1], bits_ref[2]
    result = contract(hidden_ref[...], grad_ref[...], 0, 0)
    rows, columns = result.shape[0] // 2, result.shape[1] // 2

    def put(out_ref):
        for side in range(2):
            for part in range(2):
                out_ref[side ^ x, part ^ z] = result[
                    part * rows : (part + 1) * rows, side * columns : (side + 1) * columns
                ].astype(LOW)

    @pl.when(pl.program_id(0) == 0)
    def _():
        put(sent_ref)

    @pl.when(pl.program_id(0) == 1)
    def _():
        put(kept_ref)


def in_pieces(bits, hidden_low, grad):
    rows, width = hidden_low.shape
    hidden = grad.shape[1]
    piece = (2, 2, width // 2, hidden // 4)
    return pl.pallas_call(
        in_kernel,
        grid_spec=pltpu.PrefetchScalarGridSpec(
            num_scalar_prefetch=1,
            grid=(2,),
            in_specs=[
                pl.BlockSpec((rows, width), lambda i, s: (0, 0)),
                pl.BlockSpec((rows, hidden // 2), lambda i, s: (0, s[0] ^ (1 - i))),
            ],
            out_specs=[pl.BlockSpec(piece, lambda i, s: (0, 0, 0, 0))] * 2,
        ),
        out_shape=[jax.ShapeDtypeStruct(piece, LOW)] * 2,
        cost_estimate=small_cost(),
        name="in_pieces",
    )(bits, hidden_low, grad)


def heads_kernel(bits_ref, x_ref, grads_ref, context_ref, attended_ref, sent_ref, kept_ref, scratch):
    core = bits_ref[0]
    mine = bits_ref[1] * 2 + bits_ref[2]
    extent, local = scratch.shape[1:]

    @pl.when(pl.program_id(0) < 3)
    def _():
        result = contract(x_ref[...], grads_ref[0], 0, 0)
        for part in range(8):
            scratch[part] = result[part * extent : (part + 1) * extent]

    @pl.when(pl.program_id(0) == 3)
    def _():
        result = contract(context_ref[...], attended_ref[...], 0, 0)
        for part in range(8):
            rows, side = part % 4, part // 4
            scratch[part] = result[rows * extent : (rows + 1) * extent, side * local : (side + 1) * local]

    for part in range(4):
        sent_ref[part ^ mine, 0] = scratch[(1 - core) * 4 + part].astype(LOW)
        kept_ref[part ^ mine, 0] = scratch[core * 4 + part].astype(LOW)


def heads_pieces(bits, tokens, grads, context, attended):
    rows, width = tokens.shape
    local = context.shape[1]
    return pl.pallas_call(
        heads_kernel,
        grid_spec=pltpu.PrefetchScalarGridSpec(
            num_scalar_prefetch=1,
            grid=(4,),
            in_specs=[
                pl.BlockSpec((rows, width), lambda j, s: (0, 0)),
                pl.BlockSpec((1, rows, local), lambda j, s: (jnp.minimum(j, 2), 0, 0)),
                pl.BlockSpec((rows, local), lambda j, s: (0, 0)),
                pl.BlockSpec((rows, width), lambda j, s: (0, 0)),
            ],
            out_specs=[pl.BlockSpec((4, 1, width // 8, local), lambda j, s: (0, j, 0, 0))] * 2,
            scratch_shapes=[pltpu.VMEM((8, width // 8, local), WIDE)],
        ),
        out_shape=[jax.ShapeDtypeStruct((4, 4, width // 8, local), LOW)] * 2,
        cost_estimate=small_cost(),
        name="heads_pieces",
    )(bits, tokens, grads, context, attended)


def add(*arrays):
    total = arrays[0].astype(WIDE)
    for array in arrays[1:]:
        total = total + array.astype(WIDE)
    return total.astype(LOW)


def sum_pieces(own, other, size):
    arrived = across(add(other[1], swap(other[0], 0, size)))
    chip = swap(own[0], 0, size)
    there = swap(add(own[1][1], chip[1], arrived[1]), 1, size)
    next_there = swap(add(own[1][0, 1], chip[0, 1], arrived[0, 1], there[1]), 2, size)
    kept = add(own[1][0, 0], chip[0, 0], arrived[0, 0], there[0], next_there)
    for bit in range(3, size.bit_length() - 1):
        kept = add(kept, swap(kept, bit, size))
    pieces = [kept]
    for bit in (2, 1, 0):
        pieces = pieces + [swap(piece, bit, size) for piece in pieces]
    return pieces


def widen_kernel(bits_ref, *refs):
    for index in range(8):

        @pl.when(pl.program_id(0) == index)
        def _():
            refs[-1][...] = refs[index][...].astype(WIDE)


def widen(bits, pieces, shape, block, place):
    def out_place(r, s):
        q = r ^ (s[0] * 4 + s[1] * 2 + s[2])
        return place(q // 4, (q // 2) % 2, q % 2)

    piece = pieces[0].shape
    return pl.pallas_call(
        widen_kernel,
        grid_spec=pltpu.PrefetchScalarGridSpec(
            num_scalar_prefetch=1,
            grid=(8,),
            in_specs=[pl.BlockSpec(piece, lambda r, s: (0,) * len(piece))] * 8,
            out_specs=pl.BlockSpec(block, out_place),
        ),
        out_shape=jax.ShapeDtypeStruct(shape, WIDE),
        name="widen",
    )(bits, *pieces)


def widen_heads_kernel(bits_ref, *refs):
    for index in range(8):

        @pl.when(pl.program_id(0) == index)
        def _():
            refs[-2][...] = refs[index][:3].astype(WIDE)
            refs[-1][...] = refs[index][3].astype(WIDE)


def widen_heads(bits, pieces, width, local):
    def bits_of(r, s):
        q = r ^ (s[0] * 4 + s[1] * 2 + s[2])
        return q // 4, q % 4

    piece = pieces[0].shape
    return pl.pallas_call(
        widen_heads_kernel,
        grid_spec=pltpu.PrefetchScalarGridSpec(
            num_scalar_prefetch=1,
            grid=(8,),
            in_specs=[pl.BlockSpec(piece, lambda r, s: (0,) * len(piece))] * 8,
            out_specs=[
                pl.BlockSpec((3,) + piece[1:], lambda r, s: (0, bits_of(r, s)[0] * 4 + bits_of(r, s)[1], 0)),
                pl.BlockSpec(piece[1:], lambda r, s: (bits_of(r, s)[1], bits_of(r, s)[0])),
            ],
        ),
        out_shape=[
            jax.ShapeDtypeStruct((3, width, local), WIDE),
            jax.ShapeDtypeStruct((local, width), WIDE),
        ],
        name="widen_heads",
    )(bits, *pieces)


def body(
    tokens,
    lengths,
    w_qkv,
    q_bias,
    v_bias,
    w_out,
    out_bias,
    gain_one,
    shift_one,
    w_in,
    in_bias,
    w_down,
    down_bias,
    gain_two,
    shift_two,
    cotangent,
):
    rows, width = cotangent.shape
    seq_len = tokens.shape[0] // lengths.shape[0]
    sequences = rows // seq_len
    local = w_qkv.shape[2]
    hidden = w_in.shape[1]
    size = lax.axis_size("dp")
    pair = lax.axis_index("tensor")
    dp = lax.axis_index("dp")
    bits = jnp.stack(halves(dp)).astype(jnp.int32)
    rank = (dp & 1) * 4 + ((dp >> 1) & 1) * 2 + ((dp >> 2) & 1)

    def row(vector):
        return vector.reshape(1, -1)

    def eighth(array, axis):
        extent = array.shape[axis] // 8
        return lax.dynamic_slice_in_dim(array, rank * extent, extent, axis)

    def stacked(array):
        columns = array.shape[1] // 2
        return jnp.concatenate([array[:, :columns], array[:, columns:]], axis=0)

    qkv_own = jnp.transpose(w_qkv, (1, 0, 2))
    attention_pieces = fetch(
        jnp.concatenate([eighth(qkv_own, 1), stacked(eighth(w_out, 0))[None]], axis=0), size
    )
    biases = jnp.concatenate([q_bias, v_bias, in_bias])
    biases_other = across(biases)
    forward_pieces = fetch(
        jnp.concatenate([stacked(eighth(w_in, 0)), eighth(w_down, 0)], axis=0), size
    )

    x = lax.dynamic_slice_in_dim(tokens, pair * rows, rows, 0)
    own_lengths = lax.dynamic_slice_in_dim(lengths, pair * sequences, sequences, 0)

    q_own, k_own, v_own = project(bits, x, 0, rows, local, row(biases[: 2 * local]), [qkv_own])
    context_own, probs_own = attend(own_lengths, q_own, k_own, v_own)
    q_other, k_other, v_other = project(
        bits, x, 0, rows, local, row(biases_other[: 2 * local]), attention_pieces
    )
    context_other, probs_other = attend(own_lengths, q_other, k_other, v_other)

    hidden_low, normed_one, scale_one, base, act_own, slope_own = first_half(
        bits,
        context_own,
        context_other,
        x,
        [row(out_bias), row(gain_one), row(shift_one), row(down_bias)],
        row(in_bias),
        w_out,
        w_in,
        w_down,
        attention_pieces,
    )
    (
        output,
        branch_grad,
        act_other,
        grad_own,
        grad_other,
        attended_grad,
        context_grad_own,
        context_grad_other,
        sums,
        bias_sums,
    ) = second_half(
        bits,
        hidden_low,
        base,
        cotangent,
        slope_own,
        normed_one,
        scale_one,
        [row(gain_one), row(gain_two), row(shift_two)],
        row(biases_other[2 * local :]),
        w_out,
        w_in,
        w_down,
        attention_pieces,
        forward_pieces,
    )

    down_grads = sum_pieces(
        down_pieces(bits, act_own, branch_grad), down_pieces(bits, act_other, branch_grad), size
    )
    in_grads = sum_pieces(
        in_pieces(bits, hidden_low, grad_own), in_pieces(bits, hidden_low, grad_other), size
    )

    def sum_vectors(shared, own, other):
        count = shared.shape[0]
        arrived = across(jnp.concatenate([shared, other]))
        total = jnp.concatenate([shared, own]) + arrived
        for bit in range(size.bit_length() - 1):
            total = total + swap(total, bit, size)
        return total[:count], total[count:]

    shared, grad_in_bias = sum_vectors(sums[:6].reshape(-1), bias_sums[0], bias_sums[1])
    shared = shared.reshape(6, width)

    def heads_back(q, k, v, context, context_grad, probs):
        grads = attend_back(q, k, v, context, context_grad, probs, sequences)
        pieces = heads_pieces(bits, x, grads, context, attended_grad)
        return grads, [piece.reshape(2, 2, *piece.shape[1:]) for piece in pieces]

    project_other, heads_other = heads_back(
        q_other, k_other, v_other, context_other, context_grad_other, probs_other
    )
    project_own, heads_own = heads_back(q_own, k_own, v_own, context_own, context_grad_own, probs_own)
    heads_grads = sum_pieces(heads_own, heads_other, size)

    def head_sums(grads):
        return jnp.concatenate(
            [jnp.sum(grads[0].astype(WIDE), axis=0), jnp.sum(grads[2].astype(WIDE), axis=0)]
        )

    _, head_biases = sum_vectors(
        jnp.zeros((0,), WIDE), head_sums(project_own), head_sums(project_other)
    )

    input_grad = project_back(bits, project_own, project_other, attended_grad, qkv_own, attention_pieces)

    grad_w_down = widen(
        bits, down_grads, (hidden, width), down_grads[0].shape, lambda c, i, z: (c * 4 + i * 2 + z, 0)
    )
    grad_w_in = widen(
        bits, in_grads, (width, hidden), in_grads[0].shape, lambda c, i, z: (z, c * 2 + i)
    )
    grad_qkv, grad_w_out = widen_heads(bits, heads_grads, width, local)

    return (
        output,
        input_grad,
        jnp.transpose(grad_qkv, (1, 0, 2)),
        head_biases[:local],
        head_biases[local:],
        grad_w_out,
        shared[0],
        shared[1],
        shared[2],
        grad_w_in,
        grad_in_bias,
        grad_w_down,
        shared[3],
        shared[4],
        shared[5],
    )


def solution(mesh):
    placed = (
        P("dp", None),
        P("dp"),
        P(None, None, "tensor"),
        P("tensor"),
        P("tensor"),
        P("tensor", None),
        P(),
        P(),
        P(),
        P(None, "tensor"),
        P("tensor"),
        P("tensor", None),
        P(),
        P(),
        P(),
        P(("dp", "tensor"), None),
    )
    return jax.shard_map(
        body,
        mesh=mesh,
        in_specs=placed,
        out_specs=(
            P(("dp", "tensor"), None),
            P(("dp", "tensor"), None),
            P(None, None, "tensor"),
            P("tensor"),
            P("tensor"),
            P("tensor", None),
            P(),
            P(),
            P(),
            P(None, "tensor"),
            P("tensor"),
            P("tensor", None),
            P(),
            P(),
            P(),
        ),
        check_vma=False,
    )
```

time: 476 us -> 474 us (level)
  matrix products: 119 us -> 0 us
  waiting for transfers between devices: 131 us -> 199 us
  Pallas kernels: 130 us -> 194 us
  other arithmetic: 23.1 us -> 13.1 us
  local copies, waits for them, and re-layouts: 20.5 us -> 15.2 us
  starting transfers between devices: 46.9 us -> 42 us
    dot_general x24 -> x0, matrix products: 119 us -> none  [the longest x12 48 us: contract(): lax.dot_general(a, b, (((dim_a,), (dim_b,)), ((), ())), preferred_element...]
    pallas_call x4 -> x7, Pallas kernels: 21.5 us -> 101 us  [the longest x1 39.3 us: second_half(): pl.pallas_call(second_kernel, grid_spec=pltpu.PrefetchScalarGridSpec(num_...]
    ppermute x48 -> x58, waiting for transfers between devices: 56.8 us -> 112 us  [swap(): return lax.ppermute(array, 'dp', [(i, i ^ 1 << bit) for i in range(size)])]
    ppermute x10 -> x8, waiting for transfers between devices: 74.1 us -> 87.7 us  [across(): return lax.ppermute(array, 'tensor', [(0, 1), (1, 0)])]
    reduce_sum x7 -> x2, other arithmetic: 9.99 us -> 0.55 us  [head_sums(): jnp.sum(grads[0].astype(WIDE), axis=0)]
    pallas_call x4 -> x2, Pallas kernels: 25.9 us -> 16.7 us  [heads_pieces(): pl.pallas_call(heads_kernel, grid_spec=pltpu.PrefetchScalarGridSpec(num_s...]
    unnamed x132 -> x86, local copies, waits for them, and re-layouts: 9.19 us -> 0.92 us
    reshape x0 -> x11, local copies, waits for them, and re-layouts: none -> 5.86 us  [the longest x10 5.86 us: row(): return vector.reshape(1, -1)]
  transfers between devices with their start and end apart: 58 -> 66, of which waited for: 18 -> 28; matrix products, arithmetic and copies ran while one was open for 20% -> 5% of each run, Pallas kernels for 18% -> 28%
where the time goes in v2:
time: 474 us; the launch traced here: 466 us
  waiting for transfers between devices  199 us (42%)
  Pallas kernels  194 us (41%)
  starting transfers between devices  42 us (9%)
  local copies, waits for them, and re-layouts  15.2 us (3%)
  other arithmetic  13.1 us (3%)
    ppermute x58, waiting for transfers between devices, swap(): return lax.ppermute(array, 'dp', [(i, i ^ 1 << bit) for i in range(size)])  112 us
    ppermute x8, waiting for transfers between devices, across(): return lax.ppermute(array, 'tensor', [(0, 1), (1, 0)])  87.7 us
    pallas_call x1, Pallas kernels, second_half(): pl.pallas_call(second_kernel, grid_spec=pltpu.PrefetchScalarGridSpec(num_...  39.3 us
    ppermute x58, starting transfers between devices, swap(): return lax.ppermute(array, 'dp', [(i, i ^ 1 << bit) for i in range(size)])  30.6 us
    pallas_call x2, Pallas kernels, attend_back(): pl.pallas_call(attend_back_kernel, grid=(sequences, pairs), in_specs=[blo...  22.3 us
    pallas_call x2, Pallas kernels, attend(): pl.pallas_call(attend_kernel, grid_spec=pltpu.PrefetchScalarGridSpec(num_...  21.1 us
    pallas_call x1, Pallas kernels, first_half(): pl.pallas_call(first_kernel, grid_spec=pltpu.PrefetchScalarGridSpec(num_s...  20.4 us
    pallas_call x2, Pallas kernels, heads_pieces(): pl.pallas_call(heads_kernel, grid_spec=pltpu.PrefetchScalarGridSpec(num_s...  16.7 us
  transfers between devices with their start and end apart: 66, of which 28 were waited for; matrix products, arithmetic and copies ran while one was open for 5% of the time, Pallas kernels for 28%

profile of v2, /device:TPU:0, one launch (start us, length us, event | category | flops | bytes accessed | tf_op | source)
XLA Modules:
  0.0 466.0 jit_solution(6640565483636218069)
XLA Ops:
  3.8 3.0 collective-permute-start.9
  7.6 12.8 %collective-permute-done.9.refs_8_ = bf16[384,768]{1,0:T(8,128)(2,1)} collective-permute-done((bf16[384,768]{1,0:T(8,128)(2,1)}, bf16[384,768]{1,0:T(8,128)(2,1)}, u32[]{:S(2)}, u32[]{:S(2)}) %collective-permute-start.9) | collective-permute-done | bytes 589856 | tf_op jit(solution)/shard_map/ppermute | solution.py:31
  20.4 1.8 collective-permute-start.10
  24.8 6.1 %collective-permute-done.1.refs_0_ = bf16[4,96,384]{2,1,0:T(8,128)(2,1)S(1)} collective-permute-done((bf16[4,96,384]{2,1,0:T(8,128)(2,1)S(1)}, bf16[4,96,384]{2,1,0:T(8,128)(2,1)S(1)}, u32[]{:S(2)}, u32[]{:S(2)}) %collective-permute-start.1) | collective-permute-done | bytes 294944 | tf_op jit(solution)/shard_map/ppermute | solution.py:31
  33.5 3.5 collective-permute-done.10.refs_9_
  40.3 2.2 collective-permute-done
  45.1 8.5 %collective-permute-done.11.refs_10_ = bf16[384,768]{1,0:T(8,128)(2,1)} collective-permute-done((bf16[384,768]{1,0:T(8,128)(2,1)}, bf16[384,768]{1,0:T(8,128)(2,1)}, u32[]{:S(2)}, u32[]{:S(2)}) %collective-permute-start.11) | collective-permute-done | bytes 589856 | tf_op jit(solution)/shard_map/ppermute | solution.py:27
  53.6 12.6 %collective-permute-done.12.refs_11_ = bf16[384,768]{1,0:T(8,128)(2,1)} collective-permute-done((bf16[384,768]{1,0:T(8,128)(2,1)}, bf16[384,768]{1,0:T(8,128)(2,1)}, u32[]{:S(2)}, u32[]{:S(2)}) %collective-permute-start.12) | collective-permute-done | bytes 589856 | tf_op jit(solution)/shard_map/ppermute | solution.py:27
  66.2 3.2 collective-permute-done.4.refs_3_
  76.7 7.4 %project.2 = (bf16[1024,384]{1,0:T(8,128)(2,1)}, bf16[1024,384]{1,0:T(8,128)(2,1)}, bf16[1024,384]{1,0:T(8,128)(2,1)}) custom-call(s32[3]{0:T(128)} %pad_add_fusion.bits_ref, bf16[1024,768]{1,0:T(8,128)(2,1)} %constant_dynamic-slice_fusion.3.x_ref, f32[1,768]{1,0:T(1,128)} %reshape.153.q_bias_ref.v_bias_ref, f32[1,768]{1,0:T(1,128)} %reshape.153.q_bias_ref.v_bias_ref, ...), custom_call_target="tpu_custom_call" | custom-call | flops 1000000 | bytes 100000 | tf_op jit(solution)/shard_map/project/pallas_call | solution.py:226
  84.1 10.6 %attend.2 = (bf16[1024,384]{1,0:T(8,128)(2,1)}, bf16[12,512,512]{2,1,0:T(8,128)(2,1)}) custom-call(s32[2]{0:T(128)} %dynamic_slice.18.length_ref, bf16[1024,384]{1,0:T(8,128)(2,1)} %get-tuple-element.55.q_ref, bf16[1024,384]{1,0:T(8,128)(2,1)} %get-tuple-element.56.k_ref, bf16[1024,384]{1,0:T(8,128)(2,1)} %get-tuple-element.57.v_ref), custom_call_target="tpu_custom_call" | custom-call | flops 1000000 | bytes 100000 | tf_op jit(solution)/shard_map/attend/pallas_call | solution.py:63
  95.8 7.4 %project.3 = (bf16[1024,384]{1,0:T(8,128)(2,1)}, bf16[1024,384]{1,0:T(8,128)(2,1)}, bf16[1024,384]{1,0:T(8,128)(2,1)}) custom-call(s32[3]{0:T(128)} %pad_add_fusion.bits_ref, bf16[1024,768]{1,0:T(8,128)(2,1)} %constant_dynamic-slice_fusion.3.x_ref, f32[1,768]{1,0:T(1,128)} %reshape.154.q_bias_ref.v_bias_ref, f32[1,768]{1,0:T(1,128)} %reshape.154.q_bias_ref.v_bias_ref, ...), custom_call_target="tpu_custom_call" | custom-call | flops 1000000 | bytes 100000 | tf_op jit(solution)/shard_map/project/pallas_call | solution.py:226
  103.2 10.6 %attend.3 = (bf16[1024,384]{1,0:T(8,128)(2,1)}, bf16[12,512,512]{2,1,0:T(8,128)(2,1)}) custom-call(s32[2]{0:T(128)} %dynamic_slice.18.length_ref, bf16[1024,384]{1,0:T(8,128)(2,1)} %get-tuple-element.59.q_ref, bf16[1024,384]{1,0:T(8,128)(2,1)} %get-tuple-element.60.k_ref, bf16[1024,384]{1,0:T(8,128)(2,1)} %get-tuple-element.61.v_ref), custom_call_target="tpu_custom_call" | custom-call | flops 1000000 | bytes 100000 | tf_op jit(solution)/shard_map/attend/pallas_call | solution.py:63
  113.8 20.4 %first_half.1 = (bf16[1024,768]{1,0:T(8,128)(2,1)}, bf16[1024,768]{1,0:T(8,128)(2,1)}, f32[1024,1]{1,0:T(8,128)}, f32[1024,768]{1,0:T(8,128)}, bf16[1024,1536]{1,0:T(8,128)(2,1)}, /*index=5*/bf16[1024,1536]{1,0:T(8,128)(2,1)}) custom-call(s32[3]{0:T(128)} %pad_add_fusion.bits_ref, bf16[1024,384]{1,0:T(8,128)(2,1)} %get-tuple-element.58.own_context_ref.context_ref, ...), custom_call_target="tpu_custom_call" | custom-call | flops 1000000 | bytes 100000 | tf_op jit(solution)/shard_map/first_half/pallas_call | solution.py:373
  134.2 39.3 %second_half.1 = (bf16[1024,768]{1,0:T(8,128)(2,1)}, bf16[1024,768]{1,0:T(8,128)(2,1)}, bf16[1024,1536]{1,0:T(8,128)(2,1)}, bf16[1024,1536]{1,0:T(8,128)(2,1)}, ...) custom-call(s32[3]{0:T(128)} %pad_add_fusion.bits_ref, ...), custom_call_target="tpu_custom_call" | custom-call | flops 1000000 | bytes 100000 | tf_op jit(solution)/shard_map/second_half/pallas_call | solution.py:502
  173.5 11.1 %attend_back.3.other_ref.grads_ref = bf16[3,1024,384]{2,1,0:T(8,128)(2,1)} custom-call(bf16[1024,384]{1,0:T(8,128)(2,1)} %get-tuple-element.59.q_ref, bf16[1024,384]{1,0:T(8,128)(2,1)} %get-tuple-element.60.k_ref, bf16[1024,384]{1,0:T(8,128)(2,1)} %get-tuple-element.61.v_ref, bf16[1024,384]{1,0:T(8,128)(2,1)} %get-tuple-element.62.other_context_ref.context_ref, ...), custom_call_target="tpu_custom_call" | custom-call | flops 1000000 | bytes 100000 | tf_op jit(solution)/shard_map/attend_back/pallas_call | solution.py:107
  184.6 8.3 %heads_pieces.3 = (bf16[4,4,96,384]{3,2,1,0:T(8,128)(2,1)}, bf16[4,4,96,384]{3,2,1,0:T(8,128)(2,1)}) custom-call(s32[3]{0:T(128)} %pad_add_fusion.bits_ref, bf16[1024,768]{1,0:T(8,128)(2,1)} %constant_dynamic-slice_fusion.3.x_ref, bf16[3,1024,384]{2,1,0:T(8,128)(2,1)} %attend_back.3.other_ref.grads_ref, ...), custom_call_target="tpu_custom_call" | custom-call | flops 1000000 | bytes 100000 | tf_op jit(solution)/shard_map/heads_pieces/pallas_call | solution.py:669
  193.4 7.1 %in_pieces.3 = (bf16[2,2,384,384]{3,2,1,0:T(8,128)(2,1)}, bf16[2,2,384,384]{3,2,1,0:T(8,128)(2,1)}) custom-call(s32[3]{0:T(128)} %pad_add_fusion.bits_ref, bf16[1024,768]{1,0:T(8,128)(2,1)} %get-tuple-element.63.hidden_ref, bf16[1024,1536]{1,0:T(8,128)(2,1)} %get-tuple-element.85.grad_ref), custom_call_target="tpu_custom_call" | custom-call | flops 1000000 | bytes 100000 | tf_op jit(solution)/shard_map/in_pieces/pallas_call | solution.py:626
  200.6 7.6 %down_pieces.3 = (bf16[2,2,192,768]{3,2,1,0:T(8,128)(2,1)}, bf16[2,2,192,768]{3,2,1,0:T(8,128)(2,1)}) custom-call(s32[3]{0:T(128)} %pad_add_fusion.bits_ref, bf16[1024,1536]{1,0:T(8,128)(2,1)} %get-tuple-element.92.act_ref, bf16[1024,768]{1,0:T(8,128)(2,1)} %get-tuple-element.89.grad_ref), custom_call_target="tpu_custom_call" | custom-call | flops 1000000 | bytes 100000 | tf_op jit(solution)/shard_map/down_pieces/pallas_call | solution.py:579
  211.2 11.2 %attend_back.2.own_ref.grads_ref = bf16[3,1024,384]{2,1,0:T(8,128)(2,1)} custom-call(bf16[1024,384]{1,0:T(8,128)(2,1)} %get-tuple-element.55.q_ref, bf16[1024,384]{1,0:T(8,128)(2,1)} %get-tuple-element.56.k_ref, bf16[1024,384]{1,0:T(8,128)(2,1)} %get-tuple-element.57.v_ref, bf16[1024,384]{1,0:T(8,128)(2,1)} %get-tuple-element.58.own_context_ref.context_ref, ...), custom_call_target="tpu_custom_call" | custom-call | flops 1000000 | bytes 100000 | tf_op jit(solution)/shard_map/attend_back/pallas_call | solution.py:107
  222.4 8.4 %heads_pieces.2 = (bf16[4,4,96,384]{3,2,1,0:T(8,128)(2,1)}, bf16[4,4,96,384]{3,2,1,0:T(8,128)(2,1)}) custom-call(s32[3]{0:T(128)} %pad_add_fusion.bits_ref, bf16[1024,768]{1,0:T(8,128)(2,1)} %constant_dynamic-slice_fusion.3.x_ref, bf16[3,1024,384]{2,1,0:T(8,128)(2,1)} %attend_back.2.own_ref.grads_ref, ...), custom_call_target="tpu_custom_call" | custom-call | flops 1000000 | bytes 100000 | tf_op jit(solution)/shard_map/heads_pieces/pallas_call | solution.py:669
  231.4 7.5 %down_pieces.2 = (bf16[2,2,192,768]{3,2,1,0:T(8,128)(2,1)}, bf16[2,2,192,768]{3,2,1,0:T(8,128)(2,1)}) custom-call(s32[3]{0:T(128)} %pad_add_fusion.bits_ref, bf16[1024,1536]{1,0:T(8,128)(2,1)} %get-tuple-element.88.act_ref, bf16[1024,768]{1,0:T(8,128)(2,1)} %get-tuple-element.89.grad_ref), custom_call_target="tpu_custom_call" | custom-call | flops 1000000 | bytes 100000 | tf_op jit(solution)/shard_map/down_pieces/pallas_call | solution.py:579
  238.8 7.2 %in_pieces.2 = (bf16[2,2,384,384]{3,2,1,0:T(8,128)(2,1)}, bf16[2,2,384,384]{3,2,1,0:T(8,128)(2,1)}) custom-call(s32[3]{0:T(128)} %pad_add_fusion.bits_ref, bf16[1024,768]{1,0:T(8,128)(2,1)} %get-tuple-element.63.hidden_ref, bf16[1024,1536]{1,0:T(8,128)(2,1)} %get-tuple-element.82.grad_ref), custom_call_target="tpu_custom_call" | custom-call | flops 1000000 | bytes 100000 | tf_op jit(solution)/shard_map/in_pieces/pallas_call | solution.py:626
  249.9 1.7 add_convert_fusion.1
  253.3 1.7 add_convert_fusion
  256.7 21.5 %collective-permute-done.19 = bf16[2,2,4,96,384]{4,3,2,1,0:T(8,128)(2,1)S(1)} collective-permute-done((bf16[2,2,4,96,384]{4,3,2,1,0:T(8,128)(2,1)S(1)}, bf16[2,2,4,96,384]{4,3,2,1,0:T(8,128)(2,1)S(1)}, u32[]{:S(2)}, u32[]{:S(2)}) %collective-permute-start.19) | collective-permute-done | bytes 1179680 | tf_op jit(solution)/shard_map/ppermute | solution.py:31
  280.6 22.9 %collective-permute-done.42 = bf16[2,2,384,384]{3,2,1,0:T(8,128)(2,1)S(1)} collective-permute-done((bf16[2,2,384,384]{3,2,1,0:T(8,128)(2,1)S(1)}, bf16[2,2,384,384]{3,2,1,0:T(8,128)(2,1)S(1)}, u32[]{:S(2)}, u32[]{:S(2)}) %collective-permute-start.42) | collective-permute-done | bytes 1179680 | tf_op jit(solution)/shard_map/ppermute | solution.py:31
  305.8 22.3 %collective-permute-done.55 = bf16[2,2,192,768]{3,2,1,0:T(8,128)(2,1)S(1)} collective-permute-done((bf16[2,2,192,768]{3,2,1,0:T(8,128)(2,1)S(1)}, bf16[2,2,192,768]{3,2,1,0:T(8,128)(2,1)S(1)}, u32[]{:S(2)}, u32[]{:S(2)}) %collective-permute-start.55) | collective-permute-done | bytes 1179680 | tf_op jit(solution)/shard_map/ppermute | solution.py:31
  331.7 11.4 %collective-permute-done.32 = f32[768]{0:T(1024)S(1)} collective-permute-done((f32[768]{0:T(1024)S(1)}, f32[768]{0:T(1024)S(1)}, u32[]{:S(2)}, u32[]{:S(2)}) %collective-permute-start.32) | collective-permute-done | bytes 3104 | tf_op jit(solution)/shard_map/ppermute | solution.py:27
  343.5 3.2 collective-permute-done.33
  346.7 2.6 collective-permute-start.34
  353.8 10.2 %collective-permute-done.21 = bf16[4,96,384]{2,1,0:T(8,128)(2,1)S(1)} collective-permute-done((bf16[4,96,384]{2,1,0:T(8,128)(2,1)S(1)}, bf16[4,96,384]{2,1,0:T(8,128)(2,1)S(1)}, u32[]{:S(2)}, u32[]{:S(2)}) %collective-permute-start.21) | collective-permute-done | bytes 294944 | tf_op jit(solution)/shard_map/ppermute | solution.py:27
  365.8 8.0 %collective-permute-done.44 = bf16[384,384]{1,0:T(8,128)(2,1)S(1)} collective-permute-done((bf16[384,384]{1,0:T(8,128)(2,1)S(1)}, bf16[384,384]{1,0:T(8,128)(2,1)S(1)}, u32[]{:S(2)}, u32[]{:S(2)}) %collective-permute-start.44) | collective-permute-done | bytes 294944 | tf_op jit(solution)/shard_map/ppermute | solution.py:27
  374.0 3.9 collective-permute-done.57
  378.2 14.6 %collective-permute-done.22 = bf16[4,96,384]{2,1,0:T(8,128)(2,1)S(1)} collective-permute-done((bf16[4,96,384]{2,1,0:T(8,128)(2,1)S(1)}, bf16[4,96,384]{2,1,0:T(8,128)(2,1)S(1)}, u32[]{:S(2)}, u32[]{:S(2)}) %collective-permute-start.22) | collective-permute-done | bytes 294944 | tf_op jit(solution)/shard_map/ppermute | solution.py:27
  394.1 3.9 collective-permute-done.45
  398.1 3.1 collective-permute-done.58
  401.9 2.0 collective-permute-start.59
  403.9 4.3 collective-permute-done.23.refs_1_
  408.7 2.1 collective-permute-done.47.refs_2_
  411.3 3.2 collective-permute-done.46.refs_1_
  414.5 5.0 %collective-permute-done.59.refs_1_ = bf16[192,768]{1,0:T(8,128)(2,1)S(1)} collective-permute-done((bf16[192,768]{1,0:T(8,128)(2,1)S(1)}, bf16[192,768]{1,0:T(8,128)(2,1)S(1)}, u32[]{:S(2)}, u32[]{:S(2)}) %collective-permute-start.59) | collective-permute-done | bytes 294944 | tf_op jit(solution)/shard_map/ppermute | solution.py:27
  421.7 2.7 collective-permute-done.25.refs_3_
  424.9 5.8 %collective-permute-done.61.refs_3_ = bf16[192,768]{1,0:T(8,128)(2,1)S(1)} collective-permute-done((bf16[192,768]{1,0:T(8,128)(2,1)S(1)}, bf16[192,768]{1,0:T(8,128)(2,1)S(1)}, u32[]{:S(2)}, u32[]{:S(2)}) %collective-permute-start.61) | collective-permute-done | bytes 294944 | tf_op jit(solution)/shard_map/ppermute | solution.py:27
  430.8 12.1 %project_back.1 = bf16[1024,768]{1,0:T(8,128)(2,1)} custom-call(s32[3]{0:T(128)} %pad_add_fusion.bits_ref, bf16[3,1024,384]{2,1,0:T(8,128)(2,1)} %attend_back.2.own_ref.grads_ref, bf16[3,1024,384]{2,1,0:T(8,128)(2,1)} %attend_back.3.other_ref.grads_ref, bf16[1024,768]{1,0:T(8,128)(2,1)} %get-tuple-element.73.grad_ref.attended_ref, ...), custom_call_target="tpu_custom_call" | custom-call | flops 1000000 | bytes 100000 | tf_op jit(solution)/shard_map/project_back/pallas_call | solution.py:268
  446.4 6.1 %widen.3 = f32[1536,768]{1,0:T(8,128)} custom-call(s32[3]{0:T(128)} %pad_add_fusion.bits_ref, bf16[192,768]{1,0:T(8,128)(2,1)} %copy-done.11, bf16[192,768]{1,0:T(8,128)(2,1)} %copy-done.22, bf16[192,768]{1,0:T(8,128)(2,1)} %copy-done.24, bf16[192,768]{1,0:T(8,128)(2,1)} %copy-done.27, bf16[192,768]{1,0:T(8,128)(2,1)} %copy-done.23, ...), custom_call_target="tpu_custom_call" | custom-call | tf_op jit(solution)/shard_map/widen/pallas_call | solution.py:724
  453.3 6.3 %widen.2 = f32[768,1536]{1,0:T(8,128)} custom-call(s32[3]{0:T(128)} %pad_add_fusion.bits_ref, bf16[384,384]{1,0:T(8,128)(2,1)} %copy-done.10, bf16[384,384]{1,0:T(8,128)(2,1)} %copy-done.21, bf16[384,384]{1,0:T(8,128)(2,1)} %copy-done.20, bf16[384,384]{1,0:T(8,128)(2,1)} %collective-permute-done.48.refs_3_, bf16[384,384]{1,0:T(8,128)(2,1)} %copy-done.19, ...), custom_call_target="tpu_custom_call" | custom-call | tf_op jit(solution)/shard_map/widen/pallas_call | solution.py:724
  459.6 6.0 %widen_heads.1 = (f32[3,768,384]{2,1,0:T(8,128)}, f32[384,768]{1,0:T(8,128)}) custom-call(s32[3]{0:T(128)} %pad_add_fusion.bits_ref, bf16[4,96,384]{2,1,0:T(8,128)(2,1)} %add_convert_fusion.6.refs_0_, bf16[4,96,384]{2,1,0:T(8,128)(2,1)} %copy-done.29, bf16[4,96,384]{2,1,0:T(8,128)(2,1)} %collective-permute-done.24.refs_2_, bf16[4,96,384]{2,1,0:T(8,128)(2,1)} %copy-done.30, ...), custom_call_target="tpu_custom_call" | custom-call | tf_op jit(solution)/shard_map/widen_heads/pallas_call | solution.py:752
  (246 shorter events, 60.1 us)
Async XLA Ops:
  3.8 16.6 %collective-permute-start.9 = (bf16[384,768]{1,0:T(8,128)(2,1)}, bf16[384,768]{1,0:T(8,128)(2,1)}, u32[]{:S(2)}, u32[]{:S(2)}) collective-permute-start(bf16[384,768]{1,0:T(8,128)(2,1)} %pad_maximum_fusion), channel_id=1, source_target_pairs={{0,1},{1,0},{2,3},{3,2},{4,5},{5,4},{6,7},{7,6},{8,9},{9,8},{10,11... | collective-permute-start | bytes 1769480 | tf_op jit(solution)/shard_map/ppermute | solution.py:31
  20.4 16.6 %collective-permute-start.10 = (bf16[384,768]{1,0:T(8,128)(2,1)}, bf16[384,768]{1,0:T(8,128)(2,1)}, u32[]{:S(2)}, u32[]{:S(2)}) collective-permute-start(bf16[384,768]{1,0:T(8,128)(2,1)} %collective-permute-done.9.refs_8_), channel_id=1, source_target_pairs={{0,8},{2,10},{4,12},{6,14},{8,0},{10,2},{12,4},{14,6},{16,24},{18,... | collective-permute-start | bytes 1769480 | tf_op jit(solution)/shard_map/ppermute | solution.py:27
  32.8 20.7 %collective-permute-start.11 = (bf16[384,768]{1,0:T(8,128)(2,1)}, bf16[384,768]{1,0:T(8,128)(2,1)}, u32[]{:S(2)}, u32[]{:S(2)}) collective-permute-start(bf16[384,768]{1,0:T(8,128)(2,1)} %collective-permute-done.9.refs_8_), channel_id=1, source_target_pairs={{0,4},{2,6},{4,0},{6,2},{8,12},{10,14},{12,8},{14,10},{16,20},{18,... | collective-permute-start | bytes 1769480 | tf_op jit(solution)/shard_map/ppermute | solution.py:27
  37.0 29.2 %collective-permute-start.12 = (bf16[384,768]{1,0:T(8,128)(2,1)}, bf16[384,768]{1,0:T(8,128)(2,1)}, u32[]{:S(2)}, u32[]{:S(2)}) collective-permute-start(bf16[384,768]{1,0:T(8,128)(2,1)} %collective-permute-done.10.refs_9_), channel_id=1, source_target_pairs={{0,4},{2,6},{4,0},{6,2},{8,12},{10,14},{12,8},{14,10},{16,20},{18,... | collective-permute-start | bytes 1769480 | tf_op jit(solution)/shard_map/ppermute | solution.py:27
  44.1 25.3 %collective-permute-start.4 = (bf16[4,96,384]{2,1,0:T(8,128)(2,1)S(1)}, bf16[4,96,384]{2,1,0:T(8,128)(2,1)}, u32[]{:S(2)}, u32[]{:S(2)}) collective-permute-start(bf16[4,96,384]{2,1,0:T(8,128)(2,1)S(1)} %collective-permute-done.2.refs_1_), channel_id=1, source_target_pairs={{0,4},{2,6},{4,0},{6,2},{8,12},{10,14},{12,8},{14,10},{16,20},{18,... | collective-permute-start | bytes 884744 | tf_op jit(solution)/shard_map/ppermute | solution.py:27
  44.5 89.7 %collective-permute-start.13 = (bf16[384,768]{1,0:T(8,128)(2,1)}, bf16[384,768]{1,0:T(8,128)(2,1)}, u32[]{:S(2)}, u32[]{:S(2)}) collective-permute-start(bf16[384,768]{1,0:T(8,128)(2,1)} %collective-permute-done.9.refs_8_), channel_id=1, source_target_pairs={{0,2},{2,0},{4,6},{6,4},{8,10},{10,8},{12,14},{14,12},{16,18},{18,... | collective-permute-start | bytes 1769480 | tf_op jit(solution)/shard_map/ppermute | solution.py:27
  44.9 89.3 %collective-permute-start.14 = (bf16[384,768]{1,0:T(8,128)(2,1)}, bf16[384,768]{1,0:T(8,128)(2,1)}, u32[]{:S(2)}, u32[]{:S(2)}) collective-permute-start(bf16[384,768]{1,0:T(8,128)(2,1)} %collective-permute-done.10.refs_9_), channel_id=1, source_target_pairs={{0,2},{2,0},{4,6},{6,4},{8,10},{10,8},{12,14},{14,12},{16,18},{18,... | collective-permute-start | bytes 1769480 | tf_op jit(solution)/shard_map/ppermute | solution.py:27
  53.6 80.6 %collective-permute-start.15 = (bf16[384,768]{1,0:T(8,128)(2,1)}, bf16[384,768]{1,0:T(8,128)(2,1)}, u32[]{:S(2)}, u32[]{:S(2)}) collective-permute-start(bf16[384,768]{1,0:T(8,128)(2,1)} %collective-permute-done.11.refs_10_), channel_id=1, source_target_pairs={{0,2},{2,0},{4,6},{6,4},{8,10},{10,8},{12,14},{14,12},{16,18},{18,... | collective-permute-start | bytes 1769480 | tf_op jit(solution)/shard_map/ppermute | solution.py:27
  66.2 68.0 %collective-permute-start.16 = (bf16[384,768]{1,0:T(8,128)(2,1)}, bf16[384,768]{1,0:T(8,128)(2,1)}, u32[]{:S(2)}, u32[]{:S(2)}) collective-permute-start(bf16[384,768]{1,0:T(8,128)(2,1)} %collective-permute-done.12.refs_11_), channel_id=1, source_target_pairs={{0,2},{2,0},{4,6},{6,4},{8,10},{10,8},{12,14},{14,12},{16,18},{18,... | collective-permute-start | bytes 1769480 | tf_op jit(solution)/shard_map/ppermute | solution.py:27
  69.4 26.4 %collective-permute-start.8 = (bf16[4,96,384]{2,1,0:T(8,128)(2,1)}, bf16[4,96,384]{2,1,0:T(8,128)(2,1)}, u32[]{:S(2)}, u32[]{:S(2)}) collective-permute-start(bf16[4,96,384]{2,1,0:T(8,128)(2,1)} %collective-permute-done.4.refs_3_), channel_id=1, source_target_pairs={{0,2},{2,0},{4,6},{6,4},{8,10},{10,8},{12,14},{14,12},{16,18},{18,... | collective-permute-start | bytes 884744 | tf_op jit(solution)/shard_map/ppermute | solution.py:27
  192.9 53.2 %collective-permute-start.18 = (bf16[2,2,4,96,384]{4,3,2,1,0:T(8,128)(2,1)}, bf16[2,2,4,96,384]{4,3,2,1,0:T(8,128)(2,1)}, u32[]{:S(2)}, u32[]{:S(2)}) collective-permute-start(bf16[2,2,4,96,384]{4,3,2,1,0:T(8,128)(2,1)} %bitcast.78), channel_id=1, source_target_pairs={{0,2},{2,0},{4,6},{6,4},{8,10},{10,8},{12,14},{14,12},{16,18},{18,... | collective-permute-start | bytes 3538952 | tf_op jit(solution)/shard_map/ppermute | solution.py:27
  200.6 48.8 %collective-permute-start.41 = (bf16[2,2,384,384]{3,2,1,0:T(8,128)(2,1)}, bf16[2,2,384,384]{3,2,1,0:T(8,128)(2,1)}, u32[]{:S(2)}, u32[]{:S(2)}) collective-permute-start(bf16[2,2,384,384]{3,2,1,0:T(8,128)(2,1)} %get-tuple-element.87), channel_id=1, source_target_pairs={{0,2},{2,0},{4,6},{6,4},{8,10},{10,8},{12,14},{14,12},{16,18},{18,... | collective-permute-start | bytes 3538952 | tf_op jit(solution)/shard_map/ppermute | solution.py:27
  208.2 43.5 %collective-permute-start.54 = (bf16[2,2,192,768]{3,2,1,0:T(8,128)(2,1)}, bf16[2,2,192,768]{3,2,1,0:T(8,128)(2,1)S(1)}, u32[]{:S(2)}, u32[]{:S(2)}) collective-permute-start(bf16[2,2,192,768]{3,2,1,0:T(8,128)(2,1)} %get-tuple-element.94), channel_id=1, source_target_pairs={{0,2},{2,0},{4,6},{6,4},{8,10},{10,8},{12,14},{14,12},{16,18},{18,... | collective-permute-start | bytes 3538952 | tf_op jit(solution)/shard_map/ppermute | solution.py:27
  209.6 21.2 %collective-permute-start.35 = (f32[6144]{0:T(1024)S(1)}, f32[6144]{0:T(1024)S(1)}, u32[]{:S(2)}, u32[]{:S(2)}) collective-permute-start(f32[6144]{0:T(1024)S(1)} %pad_maximum_fusion.2), channel_id=1, source_target_pairs={{0,1},{1,0},{2,3},{3,2},{4,5},{5,4},{6,7},{7,6},{8,9},{9,8},{10,11... | collective-permute-start | bytes 73736 | tf_op jit(solution)/shard_map/ppermute | solution.py:31
  230.8 24.3 %collective-permute-start.17 = (bf16[2,2,4,96,384]{4,3,2,1,0:T(8,128)(2,1)}, bf16[2,2,4,96,384]{4,3,2,1,0:T(8,128)(2,1)}, u32[]{:S(2)}, u32[]{:S(2)}) collective-permute-start(bf16[2,2,4,96,384]{4,3,2,1,0:T(8,128)(2,1)} %bitcast.79), channel_id=1, source_target_pairs={{0,2},{2,0},{4,6},{6,4},{8,10},{10,8},{12,14},{14,12},{16,18},{18,... | collective-permute-start | bytes 3538952 | tf_op jit(solution)/shard_map/ppermute | solution.py:27
  230.8 15.3 %collective-permute-start.36 = (f32[6144]{0:T(1024)S(1)}, f32[6144]{0:T(1024)S(1)}, u32[]{:S(2)}, u32[]{:S(2)}) collective-permute-start(f32[6144]{0:T(1024)S(1)} %fusion.13), channel_id=1, source_target_pairs={{0,2},{2,0},{4,6},{6,4},{8,10},{10,8},{12,14},{14,12},{16,18},{18,... | collective-permute-start | bytes 73736 | tf_op jit(solution)/shard_map/ppermute | solution.py:27
  246.1 34.0 %collective-permute-start.40 = (bf16[2,2,384,384]{3,2,1,0:T(8,128)(2,1)}, bf16[2,2,384,384]{3,2,1,0:T(8,128)(2,1)S(1)}, u32[]{:S(2)}, u32[]{:S(2)}) collective-permute-start(bf16[2,2,384,384]{3,2,1,0:T(8,128)(2,1)} %get-tuple-element.84), channel_id=1, source_target_pairs={{0,2},{2,0},{4,6},{6,4},{8,10},{10,8},{12,14},{14,12},{16,18},{18,... | collective-permute-start | bytes 3538952 | tf_op jit(solution)/shard_map/ppermute | solution.py:27
  249.3 28.9 %collective-permute-start.19 = (bf16[2,2,4,96,384]{4,3,2,1,0:T(8,128)(2,1)S(1)}, bf16[2,2,4,96,384]{4,3,2,1,0:T(8,128)(2,1)S(1)}, u32[]{:S(2)}, u32[]{:S(2)}) collective-permute-start(bf16[2,2,4,96,384]{4,3,2,1,0:T(8,128)(2,1)S(1)} %fusion), channel_id=1, source_target_pairs={{0,1},{1,0},{2,3},{3,2},{4,5},{5,4},{6,7},{7,6},{8,9},{9,8},{10,11... | collective-permute-start | bytes 3538952 | tf_op jit(solution)/shard_map/ppermute | solution.py:31
  251.7 51.8 %collective-permute-start.42 = (bf16[2,2,384,384]{3,2,1,0:T(8,128)(2,1)S(1)}, bf16[2,2,384,384]{3,2,1,0:T(8,128)(2,1)S(1)}, u32[]{:S(2)}, u32[]{:S(2)}) collective-permute-start(bf16[2,2,384,384]{3,2,1,0:T(8,128)(2,1)S(1)} %add_convert_fusion.1), channel_id=1, source_target_pairs={{0,1},{1,0},{2,3},{3,2},{4,5},{5,4},{6,7},{7,6},{8,9},{9,8},{10,11... | collective-permute-start | bytes 3538952 | tf_op jit(solution)/shard_map/ppermute | solution.py:31
  255.0 49.2 %collective-permute-start.53 = (bf16[2,2,192,768]{3,2,1,0:T(8,128)(2,1)S(1)}, bf16[2,2,192,768]{3,2,1,0:T(8,128)(2,1)S(1)}, u32[]{:S(2)}, u32[]{:S(2)}) collective-permute-start(bf16[2,2,192,768]{3,2,1,0:T(8,128)(2,1)S(1)} %copy-done.41), channel_id=1, source_target_pairs={{0,2},{2,0},{4,6},{6,4},{8,10},{10,8},{12,14},{14,12},{16,18},{18,... | collective-permute-start | bytes 3538952 | tf_op jit(solution)/shard_map/ppermute | solution.py:27
  255.1 73.0 %collective-permute-start.55 = (bf16[2,2,192,768]{3,2,1,0:T(8,128)(2,1)S(1)}, bf16[2,2,192,768]{3,2,1,0:T(8,128)(2,1)S(1)}, u32[]{:S(2)}, u32[]{:S(2)}) collective-permute-start(bf16[2,2,192,768]{3,2,1,0:T(8,128)(2,1)S(1)} %add_convert_fusion), channel_id=1, source_target_pairs={{0,1},{1,0},{2,3},{3,2},{4,5},{5,4},{6,7},{7,6},{8,9},{9,8},{10,11... | collective-permute-start | bytes 3538952 | tf_op jit(solution)/shard_map/ppermute | solution.py:31
  278.2 50.7 %collective-permute-start.30 = (f32[768]{0:T(1024)S(1)}, f32[768]{0:T(1024)S(1)}, u32[]{:S(2)}, u32[]{:S(2)}) collective-permute-start(f32[768]{0:T(1024)S(1)} %pad_maximum_fusion.6), channel_id=1, source_target_pairs={{0,1},{1,0},{2,3},{3,2},{4,5},{5,4},{6,7},{7,6},{8,9},{9,8},{10,11... | collective-permute-start | bytes 9224 | tf_op jit(solution)/shard_map/ppermute | solution.py:31
  280.1 69.2 %collective-permute-start.38 = (f32[6144]{0:T(1024)S(1)}, f32[6144]{0:T(1024)S(1)}, u32[]{:S(2)}, u32[]{:S(2)}) collective-permute-start(f32[6144]{0:T(1024)S(1)} %add.206), channel_id=1, source_target_pairs={{0,8},{2,10},{4,12},{6,14},{8,0},{10,2},{12,4},{14,6},{16,24},{18,... | collective-permute-start | bytes 73736 | tf_op jit(solution)/shard_map/ppermute | solution.py:27
  303.5 46.2 %collective-permute-start.20 = (bf16[2,4,96,384]{3,2,1,0:T(8,128)(2,1)S(1)}, bf16[2,4,96,384]{3,2,1,0:T(8,128)(2,1)S(1)}, u32[]{:S(2)}, u32[]{:S(2)}) collective-permute-start(bf16[2,4,96,384]{3,2,1,0:T(8,128)(2,1)S(1)} %fusion.1), channel_id=1, source_target_pairs={{0,4},{2,6},{4,0},{6,2},{8,12},{10,14},{12,8},{14,10},{16,20},{18,... | collective-permute-start | bytes 1769480 | tf_op jit(solution)/shard_map/ppermute | solution.py:27
  304.3 47.0 %collective-permute-start.43 = (bf16[2,384,384]{2,1,0:T(8,128)(2,1)S(1)}, bf16[2,384,384]{2,1,0:T(8,128)(2,1)S(1)}, u32[]{:S(2)}, u32[]{:S(2)}) collective-permute-start(bf16[2,384,384]{2,1,0:T(8,128)(2,1)S(1)} %fusion.2), channel_id=1, source_target_pairs={{0,4},{2,6},{4,0},{6,2},{8,12},{10,14},{12,8},{14,10},{16,20},{18,... | collective-permute-start | bytes 1769480 | tf_op jit(solution)/shard_map/ppermute | solution.py:27
  328.3 24.8 %collective-permute-start.56 = (bf16[2,192,768]{2,1,0:T(8,128)(2,1)S(1)}, bf16[2,192,768]{2,1,0:T(8,128)(2,1)S(1)}, u32[]{:S(2)}, u32[]{:S(2)}) collective-permute-start(bf16[2,192,768]{2,1,0:T(8,128)(2,1)S(1)} %fusion.3), channel_id=1, source_target_pairs={{0,4},{2,6},{4,0},{6,2},{8,12},{10,14},{12,8},{14,10},{16,20},{18,... | collective-permute-start | bytes 1769480 | tf_op jit(solution)/shard_map/ppermute | solution.py:27
  330.2 12.9 %collective-permute-start.32 = (f32[768]{0:T(1024)S(1)}, f32[768]{0:T(1024)S(1)}, u32[]{:S(2)}, u32[]{:S(2)}) collective-permute-start(f32[768]{0:T(1024)S(1)} %add.200), channel_id=1, source_target_pairs={{0,4},{2,6},{4,0},{6,2},{8,12},{10,14},{12,8},{14,10},{16,20},{18,... | collective-permute-start | bytes 9224 | tf_op jit(solution)/shard_map/ppermute | solution.py:27
  346.7 54.6 %collective-permute-start.34 = (f32[768]{0:T(1024)S(1)}, f32[768]{0:T(1024)S(1)}, u32[]{:S(2)}, u32[]{:S(2)}) collective-permute-start(f32[768]{0:T(1024)S(1)} %add.202), channel_id=1, source_target_pairs={{0,16},{2,18},{4,20},{6,22},{8,24},{10,26},{12,28},{14,30},{16,0},... | collective-permute-start | bytes 9224 | tf_op jit(solution)/shard_map/ppermute | solution.py:27
  349.3 52.6 %collective-permute-start.39 = (f32[6144]{0:T(1024)S(1)}, f32[6144]{0:T(1024)S(1)}, u32[]{:S(2)}, u32[]{:S(2)}) collective-permute-start(f32[6144]{0:T(1024)S(1)} %add.207), channel_id=1, source_target_pairs={{0,16},{2,18},{4,20},{6,22},{8,24},{10,26},{12,28},{14,30},{16,0},... | collective-permute-start | bytes 73736 | tf_op jit(solution)/shard_map/ppermute | solution.py:27
  350.8 13.2 %collective-permute-start.21 = (bf16[4,96,384]{2,1,0:T(8,128)(2,1)S(1)}, bf16[4,96,384]{2,1,0:T(8,128)(2,1)S(1)}, u32[]{:S(2)}, u32[]{:S(2)}) collective-permute-start(bf16[4,96,384]{2,1,0:T(8,128)(2,1)S(1)} %fusion.10), channel_id=1, source_target_pairs={{0,8},{2,10},{4,12},{6,14},{8,0},{10,2},{12,4},{14,6},{16,24},{18,... | collective-permute-start | bytes 884744 | tf_op jit(solution)/shard_map/ppermute | solution.py:27
  351.5 22.2 %collective-permute-start.44 = (bf16[384,384]{1,0:T(8,128)(2,1)S(1)}, bf16[384,384]{1,0:T(8,128)(2,1)S(1)}, u32[]{:S(2)}, u32[]{:S(2)}) collective-permute-start(bf16[384,384]{1,0:T(8,128)(2,1)S(1)} %fusion.7), channel_id=1, source_target_pairs={{0,8},{2,10},{4,12},{6,14},{8,0},{10,2},{12,4},{14,6},{16,24},{18,... | collective-permute-start | bytes 884744 | tf_op jit(solution)/shard_map/ppermute | solution.py:27
  353.3 24.6 %collective-permute-start.57 = (bf16[192,768]{1,0:T(8,128)(2,1)S(1)}, bf16[192,768]{1,0:T(8,128)(2,1)S(1)}, u32[]{:S(2)}, u32[]{:S(2)}) collective-permute-start(bf16[192,768]{1,0:T(8,128)(2,1)S(1)} %fusion.4), channel_id=1, source_target_pairs={{0,8},{2,10},{4,12},{6,14},{8,0},{10,2},{12,4},{14,6},{16,24},{18,... | collective-permute-start | bytes 884744 | tf_op jit(solution)/shard_map/ppermute | solution.py:27
  365.1 27.7 %collective-permute-start.22 = (bf16[4,96,384]{2,1,0:T(8,128)(2,1)S(1)}, bf16[4,96,384]{2,1,0:T(8,128)(2,1)S(1)}, u32[]{:S(2)}, u32[]{:S(2)}) collective-permute-start(bf16[4,96,384]{2,1,0:T(8,128)(2,1)S(1)} %fusion.12), channel_id=1, source_target_pairs={{0,16},{2,18},{4,20},{6,22},{8,24},{10,26},{12,28},{14,30},{16,0},... | collective-permute-start | bytes 884744 | tf_op jit(solution)/shard_map/ppermute | solution.py:27
  373.9 24.1 %collective-permute-start.45 = (bf16[384,384]{1,0:T(8,128)(2,1)S(1)}, bf16[384,384]{1,0:T(8,128)(2,1)S(1)}, u32[]{:S(2)}, u32[]{:S(2)}) collective-permute-start(bf16[384,384]{1,0:T(8,128)(2,1)S(1)} %fusion.9), channel_id=1, source_target_pairs={{0,16},{2,18},{4,20},{6,22},{8,24},{10,26},{12,28},{14,30},{16,0},... | collective-permute-start | bytes 884744 | tf_op jit(solution)/shard_map/ppermute | solution.py:27
  378.1 23.1 %collective-permute-start.58 = (bf16[192,768]{1,0:T(8,128)(2,1)S(1)}, bf16[192,768]{1,0:T(8,128)(2,1)S(1)}, u32[]{:S(2)}, u32[]{:S(2)}) collective-permute-start(bf16[192,768]{1,0:T(8,128)(2,1)S(1)} %fusion.6), channel_id=1, source_target_pairs={{0,16},{2,18},{4,20},{6,22},{8,24},{10,26},{12,28},{14,30},{16,0},... | collective-permute-start | bytes 884744 | tf_op jit(solution)/shard_map/ppermute | solution.py:27
  401.9 12.6 %collective-permute-start.46 = (bf16[384,384]{1,0:T(8,128)(2,1)S(1)}, bf16[384,384]{1,0:T(8,128)(2,1)S(1)}, u32[]{:S(2)}, u32[]{:S(2)}) collective-permute-start(bf16[384,384]{1,0:T(8,128)(2,1)S(1)} %add_convert_fusion.5.refs_0_), channel_id=1, source_target_pairs={{0,8},{2,10},{4,12},{6,14},{8,0},{10,2},{12,4},{14,6},{16,24},{18,... | collective-permute-start | bytes 884744 | tf_op jit(solution)/shard_map/ppermute | solution.py:27
  401.9 17.6 %collective-permute-start.59 = (bf16[192,768]{1,0:T(8,128)(2,1)S(1)}, bf16[192,768]{1,0:T(8,128)(2,1)S(1)}, u32[]{:S(2)}, u32[]{:S(2)}) collective-permute-start(bf16[192,768]{1,0:T(8,128)(2,1)S(1)} %add_convert_fusion.4.refs_0_), channel_id=1, source_target_pairs={{0,8},{2,10},{4,12},{6,14},{8,0},{10,2},{12,4},{14,6},{16,24},{18,... | collective-permute-start | bytes 884744 | tf_op jit(solution)/shard_map/ppermute | solution.py:27
  408.2 11.9 %collective-permute-start.62 = (bf16[192,768]{1,0:T(8,128)(2,1)S(1)}, bf16[192,768]{1,0:T(8,128)(2,1)S(1)}, u32[]{:S(2)}, u32[]{:S(2)}) collective-permute-start(bf16[192,768]{1,0:T(8,128)(2,1)S(1)} %add_convert_fusion.4.refs_0_), channel_id=1, source_target_pairs={{0,2},{2,0},{4,6},{6,4},{8,10},{10,8},{12,14},{14,12},{16,18},{18,... | collective-permute-start | bytes 884744 | tf_op jit(solution)/shard_map/ppermute | solution.py:27
  410.8 13.6 %collective-permute-start.25 = (bf16[4,96,384]{2,1,0:T(8,128)(2,1)S(1)}, bf16[4,96,384]{2,1,0:T(8,128)(2,1)S(1)}, u32[]{:S(2)}, u32[]{:S(2)}) collective-permute-start(bf16[4,96,384]{2,1,0:T(8,128)(2,1)S(1)} %collective-permute-done.23.refs_1_), channel_id=1, source_target_pairs={{0,4},{2,6},{4,0},{6,2},{8,12},{10,14},{12,8},{14,10},{16,20},{18,... | collective-permute-start | bytes 884744 | tf_op jit(solution)/shard_map/ppermute | solution.py:27
  420.1 22.9 %collective-permute-start.50 = (bf16[384,384]{1,0:T(8,128)(2,1)S(1)}, bf16[384,384]{1,0:T(8,128)(2,1)S(1)}, u32[]{:S(2)}, u32[]{:S(2)}) collective-permute-start(bf16[384,384]{1,0:T(8,128)(2,1)S(1)} %collective-permute-done.46.refs_1_), channel_id=1, source_target_pairs={{0,2},{2,0},{4,6},{6,4},{8,10},{10,8},{12,14},{14,12},{16,18},{18,... | collective-permute-start | bytes 884744 | tf_op jit(solution)/shard_map/ppermute | solution.py:27
  420.1 23.5 %collective-permute-start.48 = (bf16[384,384]{1,0:T(8,128)(2,1)S(1)}, bf16[384,384]{1,0:T(8,128)(2,1)}, u32[]{:S(2)}, u32[]{:S(2)}) collective-permute-start(bf16[384,384]{1,0:T(8,128)(2,1)S(1)} %collective-permute-done.46.refs_1_), channel_id=1, source_target_pairs={{0,4},{2,6},{4,0},{6,2},{8,12},{10,14},{12,8},{14,10},{16,20},{18,... | collective-permute-start | bytes 884744 | tf_op jit(solution)/shard_map/ppermute | solution.py:27
  424.4 19.3 %collective-permute-start.64 = (bf16[192,768]{1,0:T(8,128)(2,1)S(1)}, bf16[192,768]{1,0:T(8,128)(2,1)}, u32[]{:S(2)}, u32[]{:S(2)}) collective-permute-start(bf16[192,768]{1,0:T(8,128)(2,1)S(1)} %collective-permute-done.60.refs_2_), channel_id=1, source_target_pairs={{0,2},{2,0},{4,6},{6,4},{8,10},{10,8},{12,14},{14,12},{16,18},{18,... | collective-permute-start | bytes 884744 | tf_op jit(solution)/shard_map/ppermute | solution.py:27
  424.4 19.7 %collective-permute-start.63 = (bf16[192,768]{1,0:T(8,128)(2,1)S(1)}, bf16[192,768]{1,0:T(8,128)(2,1)}, u32[]{:S(2)}, u32[]{:S(2)}) collective-permute-start(bf16[192,768]{1,0:T(8,128)(2,1)S(1)} %collective-permute-done.59.refs_1_), channel_id=1, source_target_pairs={{0,2},{2,0},{4,6},{6,4},{8,10},{10,8},{12,14},{14,12},{16,18},{18,... | collective-permute-start | bytes 884744 | tf_op jit(solution)/shard_map/ppermute | solution.py:27
  430.7 13.5 %collective-permute-start.65 = (bf16[192,768]{1,0:T(8,128)(2,1)S(1)}, bf16[192,768]{1,0:T(8,128)(2,1)}, u32[]{:S(2)}, u32[]{:S(2)}) collective-permute-start(bf16[192,768]{1,0:T(8,128)(2,1)S(1)} %collective-permute-done.61.refs_3_), channel_id=1, source_target_pairs={{0,2},{2,0},{4,6},{6,4},{8,10},{10,8},{12,14},{14,12},{16,18},{18,... | collective-permute-start | bytes 884744 | tf_op jit(solution)/shard_map/ppermute | solution.py:27
  443.0 16.5 %collective-permute-start.26 = (bf16[4,96,384]{2,1,0:T(8,128)(2,1)}, bf16[4,96,384]{2,1,0:T(8,128)(2,1)}, u32[]{:S(2)}, u32[]{:S(2)}) collective-permute-start(bf16[4,96,384]{2,1,0:T(8,128)(2,1)} %add_convert_fusion.6.refs_0_), channel_id=1, source_target_pairs={{0,2},{2,0},{4,6},{6,4},{8,10},{10,8},{12,14},{14,12},{16,18},{18,... | collective-permute-start | bytes 884744 | tf_op jit(solution)/shard_map/ppermute | solution.py:27
  443.6 16.0 %collective-permute-start.27 = (bf16[4,96,384]{2,1,0:T(8,128)(2,1)}, bf16[4,96,384]{2,1,0:T(8,128)(2,1)}, u32[]{:S(2)}, u32[]{:S(2)}) collective-permute-start(bf16[4,96,384]{2,1,0:T(8,128)(2,1)} %copy-done.29), channel_id=1, source_target_pairs={{0,2},{2,0},{4,6},{6,4},{8,10},{10,8},{12,14},{14,12},{16,18},{18,... | collective-permute-start | bytes 884744 | tf_op jit(solution)/shard_map/ppermute | solution.py:27
  443.7 15.9 %collective-permute-start.28 = (bf16[4,96,384]{2,1,0:T(8,128)(2,1)}, bf16[4,96,384]{2,1,0:T(8,128)(2,1)}, u32[]{:S(2)}, u32[]{:S(2)}) collective-permute-start(bf16[4,96,384]{2,1,0:T(8,128)(2,1)} %collective-permute-done.24.refs_2_), channel_id=1, source_target_pairs={{0,2},{2,0},{4,6},{6,4},{8,10},{10,8},{12,14},{14,12},{16,18},{18,... | collective-permute-start | bytes 884744 | tf_op jit(solution)/shard_map/ppermute | solution.py:27
  444.1 15.4 %collective-permute-start.29 = (bf16[4,96,384]{2,1,0:T(8,128)(2,1)}, bf16[4,96,384]{2,1,0:T(8,128)(2,1)}, u32[]{:S(2)}, u32[]{:S(2)}) collective-permute-start(bf16[4,96,384]{2,1,0:T(8,128)(2,1)} %copy-done.30), channel_id=1, source_target_pairs={{0,2},{2,0},{4,6},{6,4},{8,10},{10,8},{12,14},{14,12},{16,18},{18,... | collective-permute-start | bytes 884744 | tf_op jit(solution)/shard_map/ppermute | solution.py:27
  (61 other events, 1358.3 us)
